TPU v7x, 128 devices: a whole 4x4x4 slice. The times are simulated.
128 devices in a mesh: rows: 32 (over y, z_lo, x), tm: 4 (over z_hi, core).
Axes of the slice: x: 4, y: 4, z: 4 (z_hi: 2, z_lo: 2; z = z_hi * 2 + z_lo), core: 2. Of those that a mesh axis runs over, the one named last changes fastest.
Arguments:
- raw_frames: bfloat16 [320, 256, 2048], P('tm', 'rows'), may hold values from -6 to 6
- dark_frame: float32 [256, 2048], P('rows'), may hold values from -0.5 to 0.5
- flat_field: float32 [256, 2048], P('rows'), may hold values from 0.5 to 1.5
- pixel_gain: float32 [256, 2048], P('rows'), may hold values from 0.1 to 1.9
- smoothing_kernel: float32 [5, 5], replicated, may hold values from 0.05 to 0.5
- bin_labels: int32 [256, 2048], P('rows'), may hold values from 0 to 71999
- lag_list: int32 [64], replicated, may hold values from 1 to 79, as said below
Outputs:
- correlation: float32 [4608000], P(('rows', 'tm'))
Inputs may be any that keep to these rules, and one draw needn't show every extreme that they name: `lag_list`: 64 distinct lags in rising order; the first is 1 and the last 79.
All inputs are finite; a program needn't handle non-finite values.
Results may differ from a plain program's by a relative error of at most 0.0054.
Values may be sent and summed in bfloat16 or wider, within the bound.
A program may use at most 256 MiB of HBM per device.

v0:
```python
import jax
import jax.numpy as jnp
from jax import lax
from jax.sharding import PartitionSpec as P

ANG = 360
QB = 200


def padded_2(array, sides, width):
    for axis, dim in sides:
        peers, length = (lax.axis_size(axis), array.shape[dim])
        up = [(i, (i + 1) % peers) for i in range(peers - 1)]
        down = [(j, i) for i, j in up]
        last = lax.slice_in_dim(array, length - width, length, axis=dim)
        initial = lax.slice_in_dim(array, 0, width, axis=dim)
        before = lax.ppermute(last, axis, up)
        after = lax.ppermute(initial, axis, down)
        array = jnp.concatenate([before, array, after], axis=dim)
    return array


def shift_columns(values, offset):
    if offset == 0:
        return values
    zero_pad = jnp.zeros(values.shape[:-1] + (abs(offset),), values.dtype)
    if offset > 0:
        return jnp.concatenate([values[..., offset:], zero_pad], axis=-1)
    return jnp.concatenate([zero_pad, values[..., :offset]], axis=-1)


def smooth_rows(padded, kernel, row_count):
    running = jnp.zeros((padded.shape[0], row_count, padded.shape[2]), jnp.float32)
    for kernel_row in range(5):
        band_rows = padded[:, kernel_row : kernel_row + row_count, :].astype(jnp.float32)
        for kernel_col in range(5):
            running = running + kernel[kernel_row, kernel_col] * shift_columns(
                band_rows, kernel_col - 2
            )
    return running.astype(jnp.bfloat16)


def lag_sums(series, extended, lag_list, divisor):
    frame_span = series.shape[0]
    lag_groups = lag_list.reshape(-1, 8)

    def one_group(lag_group):
        lag_rows = []
        for position in range(8):
            window = lax.dynamic_slice_in_dim(extended, lag_group[position], frame_span, 0)
            lag_rows.append(
                jnp.sum(series.astype(jnp.float32) * window.astype(jnp.float32), axis=0)
            )
        return jnp.stack(lag_rows)

    lagged = lax.map(one_group, lag_groups)
    return lagged.reshape(lag_list.shape[0], -1) / divisor[:, None]


def per_device(
    raw_frames, dark_frame, flat_field, pixel_gain, smoothing_kernel, bin_labels, lag_list
):
    weighted = ((raw_frames.astype(jnp.float32) - dark_frame) * flat_field * pixel_gain).astype(
        jnp.bfloat16
    )
    padded = padded_2(weighted, (("rows", 1),), 2)
    smoothed = smooth_rows(padded, smoothing_kernel, weighted.shape[1])
    block_frames = smoothed.shape[0]
    tm_count = lax.axis_size("tm")
    frame_total = block_frames * tm_count
    divisor = frame_total - lag_list.astype(jnp.float32)
    lag_count = lag_list.shape[0]
    series = lax.all_to_all(smoothed, "tm", split_axis=2, concat_axis=0, tiled=True)
    quarter = series.shape[2]
    labels_here = lax.dynamic_slice_in_dim(bin_labels, lax.axis_index("tm") * quarter, quarter, 1)
    flat_series = series.reshape(series.shape[0], -1)
    tail_zeros = jnp.zeros((block_frames, flat_series.shape[1]), jnp.bfloat16)
    extended = jnp.concatenate([flat_series, tail_zeros], 0)
    lagged = lag_sums(flat_series, extended, lag_list, divisor)
    bin_table = jnp.zeros((lag_count, ANG * QB), jnp.float32)
    bin_table = bin_table.at[:, labels_here.reshape(-1)].add(lagged.reshape(lag_count, -1))
    owned = lax.psum_scatter(bin_table.reshape(-1), ("rows", "tm"), scatter_dimension=0, tiled=True)
    return owned


def solution(mesh):
    return jax.shard_map(
        per_device,
        mesh=mesh,
        in_specs=(
            P("tm", "rows", None),
            P("rows", None),
            P("rows", None),
            P("rows", None),
            P(),
            P("rows", None),
            P(),
        ),
        out_specs=P(("rows", "tm")),
        check_vma=False,
    )
```

profile of v0, /device:TPU:1, one launch (start us, length us, event | category | flops | bytes accessed | tf_op | source)
XLA Modules:
  0.0 744.5 jit_solution(3258186887334234050)
XLA Ops:
  6.5 3.6 multiply_convert_fusion
  10.2 4.0 collective-permute-start
  14.2 1.3 collective-permute-start.1
  15.5 5.3 fusion.27
  20.9 0.7 fusion.29
  22.3 5.4 fusion.28
  27.7 3.8 collective-permute-done.1
  31.5 4.6 fusion.13
  36.1 15.6 %fusion.18 = (f32[80,8,2046]{2,0,1:T(8,128)}, f32[80,8,2046]{2,0,1:T(8,128)}, f32[80,8,2046]{2,0,1:T(8,128)}, f32[80,8,2046]{2,0,1:T(8,128)}) fusion(f32[80,8,2048]{2,0,1:T(8,128)} %get-tuple-element.75, f32[80,8,2048]{2,0,1:T(8,128)} %get-tuple-element.76), kind=kLoop, calls=%fused_computation.41 | loop fusion | bytes 41902080 | tf_op jit(solution)/shard_map/slice | solution.py:29
  51.7 15.7 %fusion.19 = (f32[80,8,2047]{2,0,1:T(8,128)}, f32[80,8,2047]{2,0,1:T(8,128)}, f32[80,8,2047]{2,0,1:T(8,128)}, f32[80,8,2047]{2,0,1:T(8,128)}) fusion(f32[80,8,2048]{2,0,1:T(8,128)} %get-tuple-element.75, f32[80,8,2048]{2,0,1:T(8,128)} %get-tuple-element.76), kind=kLoop, calls=%fused_computation.42 | loop fusion | bytes 41922560 | tf_op jit(solution)/shard_map/slice | solution.py:29
  67.4 8.5 %fusion.23 = (f32[80,8,2047]{2,0,1:T(8,128)}, f32[80,8,2047]{2,0,1:T(8,128)}, f32[80,8,2047]{2,0,1:T(8,128)}, f32[80,8,2047]{2,0,1:T(8,128)}) fusion(f32[80,8,2048]{2,0,1:T(8,128)S(1)} %get-tuple-element.80, f32[80,8,2048]{2,0,1:T(8,128)S(1)} %get-tuple-element.79), kind=kLoop, calls=%fused_computation.46 | loop fusion | bytes 41922560 | tf_op jit(solution)/shard_map/slice | solution.py:29
  75.9 8.5 %fusion.22 = (f32[80,8,2046]{2,0,1:T(8,128)}, f32[80,8,2046]{2,0,1:T(8,128)}, f32[80,8,2046]{2,0,1:T(8,128)}, f32[80,8,2046]{2,0,1:T(8,128)}) fusion(f32[80,8,2048]{2,0,1:T(8,128)S(1)} %get-tuple-element.80, f32[80,8,2048]{2,0,1:T(8,128)S(1)} %get-tuple-element.79), kind=kLoop, calls=%fused_computation.45 | loop fusion | bytes 41902080 | tf_op jit(solution)/shard_map/slice | solution.py:29
  84.4 50.3 %add_convert_fusion = bf16[80,8,2048]{2,0,1:T(8,128)(2,1)} fusion(f32[80,8,2046]{2,0,1:T(8,128)} %get-tuple-element.116, f32[80,8,2047]{2,0,1:T(8,128)} %get-tuple-element.118, f32[80,8,2047]{2,0,1:T(8,128)} %get-tuple-element.119, f32[80,8,2046]{2,0,1:T(8,128)} %get-tuple-element.117, f32[80,8,2046]{2,0,1:T(8,128)} %get-tuple-element.68, ...), kind=kLoop, calls=%fused_computation.21 | loop fusion | flops 77332480 | bytes 111334496 | tf_op jit(solution)/shard_map/convert_element_type | solution.py:40
  134.6 6.2 copy.24
  140.9 7.1 all-to-all-start
  149.3 47.4 %all-to-all-done = bf16[80,8,2048]{0,1,2:T(8,128)(2,1)} async-done(((bf16[80,8,2048]{0,1,2:T(8,128)(2,1)}), bf16[80,8,2048]{0,1,2:T(8,128)(2,1)}, u32[]{:S(2)}, u32[]{:S(2)}) %all-to-all-start) | async-done | bytes 2621472 | tf_op jit(solution)/shard_map/all_to_all | solution.py:73
  196.7 6.7 copy.25
  203.4 1.2 copy.29
  204.9 1.1 copy-done.2
  206.1 215.6 %while.10 = (s32[]{:T(128)}, f32[8,8,4096]{2,1,0:T(8,128)}, bf16[320,4096]{1,0:T(8,128)(2,1)}, s32[8,8]{1,0:T(8,128)}, bf16[400,4096]{1,0:T(8,128)(2,1)S(1)}, /*index=5*/s32[]{:T(128)}, s32[]{:T(128)}, s32[]{:T(128)}) while((s32[]{:T(128)}, f32[8,8,4096]{2,1,0:T(8,128)}, bf16[320,4096]{1,0:T(8,128)(2,1)}, s32[8,8]{1,0:T(8,128)}, ...), condition=%wide.region_9.10_spmd, body=%wide.region_0.9_spmd.sunk | while | flops 32735256 | bytes 24249352 | solution.py:56
  206.1 0.7 constant_dynamic-slice_fusion.2
  206.8 0.7 fusion.33
  223.0 9.2 %fusion.34 = (f32[4096]{0:T(1024)S(1)}, f32[4096]{0:T(1024)S(1)}, f32[4096]{0:T(1024)S(1)}, f32[4096]{0:T(1024)S(1)}, f32[4096]{0:T(1024)S(1)}, /*index=5*/f32[4096]{0:T(1024)S(1)}, f32[4096]{0:T(1024)S(1)}, f32[4096]{0:T(1024)S(1)}) fusion(bf16[320,4096]{1,0:T(8,128)(2,1)} %get-tuple-element.201, bf16[400,4096]{1,0:T(8,128)(2,1)S(1)} %get-tuple-element.203, ...), kind=kLoop, calls=%fused_computation.16.clone.1 | loop fusion | flops 32735232 | bytes 23724064 | tf_op jit(solution)/shard_map/while/body/eval_jaxpr/reduce_sum | solution.py:52
  233.0 0.7 constant_dynamic-slice_fusion.2
  233.7 0.7 fusion.33
  250.0 9.2 %fusion.34 = (f32[4096]{0:T(1024)S(1)}, f32[4096]{0:T(1024)S(1)}, f32[4096]{0:T(1024)S(1)}, f32[4096]{0:T(1024)S(1)}, f32[4096]{0:T(1024)S(1)}, /*index=5*/f32[4096]{0:T(1024)S(1)}, f32[4096]{0:T(1024)S(1)}, f32[4096]{0:T(1024)S(1)}) fusion(bf16[320,4096]{1,0:T(8,128)(2,1)} %get-tuple-element.201, bf16[400,4096]{1,0:T(8,128)(2,1)S(1)} %get-tuple-element.203, ...), kind=kLoop, calls=%fused_computation.16.clone.1 | loop fusion | flops 32735232 | bytes 23724064 | tf_op jit(solution)/shard_map/while/body/eval_jaxpr/reduce_sum | solution.py:52
  260.0 0.7 constant_dynamic-slice_fusion.2
  260.7 0.7 fusion.33
  276.9 9.2 %fusion.34 = (f32[4096]{0:T(1024)S(1)}, f32[4096]{0:T(1024)S(1)}, f32[4096]{0:T(1024)S(1)}, f32[4096]{0:T(1024)S(1)}, f32[4096]{0:T(1024)S(1)}, /*index=5*/f32[4096]{0:T(1024)S(1)}, f32[4096]{0:T(1024)S(1)}, f32[4096]{0:T(1024)S(1)}) fusion(bf16[320,4096]{1,0:T(8,128)(2,1)} %get-tuple-element.201, bf16[400,4096]{1,0:T(8,128)(2,1)S(1)} %get-tuple-element.203, ...), kind=kLoop, calls=%fused_computation.16.clone.1 | loop fusion | flops 32735232 | bytes 23724064 | tf_op jit(solution)/shard_map/while/body/eval_jaxpr/reduce_sum | solution.py:52
  286.9 0.7 constant_dynamic-slice_fusion.2
  287.6 0.7 fusion.33
  303.8 9.2 %fusion.34 = (f32[4096]{0:T(1024)S(1)}, f32[4096]{0:T(1024)S(1)}, f32[4096]{0:T(1024)S(1)}, f32[4096]{0:T(1024)S(1)}, f32[4096]{0:T(1024)S(1)}, /*index=5*/f32[4096]{0:T(1024)S(1)}, f32[4096]{0:T(1024)S(1)}, f32[4096]{0:T(1024)S(1)}) fusion(bf16[320,4096]{1,0:T(8,128)(2,1)} %get-tuple-element.201, bf16[400,4096]{1,0:T(8,128)(2,1)S(1)} %get-tuple-element.203, ...), kind=kLoop, calls=%fused_computation.16.clone.1 | loop fusion | flops 32735232 | bytes 23724064 | tf_op jit(solution)/shard_map/while/body/eval_jaxpr/reduce_sum | solution.py:52
  313.9 0.7 constant_dynamic-slice_fusion.2
  314.5 0.7 fusion.33
  330.8 9.2 %fusion.34 = (f32[4096]{0:T(1024)S(1)}, f32[4096]{0:T(1024)S(1)}, f32[4096]{0:T(1024)S(1)}, f32[4096]{0:T(1024)S(1)}, f32[4096]{0:T(1024)S(1)}, /*index=5*/f32[4096]{0:T(1024)S(1)}, f32[4096]{0:T(1024)S(1)}, f32[4096]{0:T(1024)S(1)}) fusion(bf16[320,4096]{1,0:T(8,128)(2,1)} %get-tuple-element.201, bf16[400,4096]{1,0:T(8,128)(2,1)S(1)} %get-tuple-element.203, ...), kind=kLoop, calls=%fused_computation.16.clone.1 | loop fusion | flops 32735232 | bytes 23724064 | tf_op jit(solution)/shard_map/while/body/eval_jaxpr/reduce_sum | solution.py:52
  340.8 0.7 constant_dynamic-slice_fusion.2
  341.5 0.7 fusion.33
  357.7 9.2 %fusion.34 = (f32[4096]{0:T(1024)S(1)}, f32[4096]{0:T(1024)S(1)}, f32[4096]{0:T(1024)S(1)}, f32[4096]{0:T(1024)S(1)}, f32[4096]{0:T(1024)S(1)}, /*index=5*/f32[4096]{0:T(1024)S(1)}, f32[4096]{0:T(1024)S(1)}, f32[4096]{0:T(1024)S(1)}) fusion(bf16[320,4096]{1,0:T(8,128)(2,1)} %get-tuple-element.201, bf16[400,4096]{1,0:T(8,128)(2,1)S(1)} %get-tuple-element.203, ...), kind=kLoop, calls=%fused_computation.16.clone.1 | loop fusion | flops 32735232 | bytes 23724064 | tf_op jit(solution)/shard_map/while/body/eval_jaxpr/reduce_sum | solution.py:52
  367.8 0.7 constant_dynamic-slice_fusion.2
  384.7 9.2 %fusion.34 = (f32[4096]{0:T(1024)S(1)}, f32[4096]{0:T(1024)S(1)}, f32[4096]{0:T(1024)S(1)}, f32[4096]{0:T(1024)S(1)}, f32[4096]{0:T(1024)S(1)}, /*index=5*/f32[4096]{0:T(1024)S(1)}, f32[4096]{0:T(1024)S(1)}, f32[4096]{0:T(1024)S(1)}) fusion(bf16[320,4096]{1,0:T(8,128)(2,1)} %get-tuple-element.201, bf16[400,4096]{1,0:T(8,128)(2,1)S(1)} %get-tuple-element.203, ...), kind=kLoop, calls=%fused_computation.16.clone.1 | loop fusion | flops 32735232 | bytes 23724064 | tf_op jit(solution)/shard_map/while/body/eval_jaxpr/reduce_sum | solution.py:52
  394.7 0.7 constant_dynamic-slice_fusion.2
  411.6 9.2 %fusion.34 = (f32[4096]{0:T(1024)S(1)}, f32[4096]{0:T(1024)S(1)}, f32[4096]{0:T(1024)S(1)}, f32[4096]{0:T(1024)S(1)}, f32[4096]{0:T(1024)S(1)}, /*index=5*/f32[4096]{0:T(1024)S(1)}, f32[4096]{0:T(1024)S(1)}, f32[4096]{0:T(1024)S(1)}) fusion(bf16[320,4096]{1,0:T(8,128)(2,1)} %get-tuple-element.201, bf16[400,4096]{1,0:T(8,128)(2,1)S(1)} %get-tuple-element.203, ...), kind=kLoop, calls=%fused_computation.16.clone.1 | loop fusion | flops 32735232 | bytes 23724064 | tf_op jit(solution)/shard_map/while/body/eval_jaxpr/reduce_sum | solution.py:52
  421.7 1.4 fusion.16
  423.6 36.8 %scatter_custom_fusion = f32[64,72000]{0,1:T(8,128)} fusion(s32[4096]{0:T(1024)S(1)} %bitcast.107, f32[4096,64]{1,0:T(8,128)S(1)} %copy.26, f32[]{:T(128)} %constant.3.clone.1), kind=kCustom, calls=%fused_computation.19 | custom fusion | flops 262144 | bytes 18432004 | tf_op jit(solution)/shard_map/scatter-add | solution.py:81
  460.5 27.3 %copy.27 = f32[64,72000]{1,0:T(8,128)} copy(f32[64,72000]{0,1:T(8,128)} %scatter_custom_fusion) | data formatting | bytes 36864000 | tf_op jit(solution)/shard_map/scatter-add | solution.py:81
  487.8 26.6 %reshape.68 = f32[4608000]{0:T(1024)} reshape(f32[64,72000]{1,0:T(8,128)} %copy.27) | data formatting | bytes 36864000 | tf_op jit(solution)/shard_map/reshape | solution.py:82
  514.4 221.5 %all-reduce.24.cloned.1.call-done = f32[4608000]{0:T(1024)} async-done(((f32[4608000]{0:T(1024)}), f32[4608000]{0:T(1024)}) %all-reduce.24.cloned.1.call-update) | async-done | bytes 18432016
  736.0 1.7 dynamic-slice
  (42 shorter events, 11.3 us)
Async XLA Ops:
  6.5 142.1 %copy-start = (s32[8,2048]{1,0:T(8,128)S(1)}, s32[8,2048]{1,0:T(8,128)}, u32[]{:S(2)}) copy-start(s32[8,2048]{1,0:T(8,128)} %param.14) | copy-start | bytes 196612
  10.2 17.4 %collective-permute-start = (bf16[80,2,2048]{2,0,1:T(8,128)(2,1)S(1)}, bf16[80,2,2048]{2,0,1:T(8,128)(2,1)S(1)}, u32[]{:S(2)}, u32[]{:S(2)}) collective-permute-start(bf16[80,2,2048]{2,0,1:T(8,128)(2,1)S(1)} %get-tuple-element.81), channel_id=1, source_target_pairs={{0,4},{4,8},{8,12},{12,16},{16,20},{20,24},{24,28},{28,32},{32,36}... | collective-permute-start | bytes 1966088 | tf_op jit(solution)/shard_map/ppermute | solution.py:17
  14.2 6.7 copy-start.4
  14.2 17.2 %collective-permute-start.1 = (bf16[80,2,2048]{2,0,1:T(8,128)(2,1)S(1)}, bf16[80,2,2048]{2,0,1:T(8,128)(2,1)S(1)}, u32[]{:S(2)}, u32[]{:S(2)}) collective-permute-start(bf16[80,2,2048]{2,0,1:T(8,128)(2,1)S(1)} %get-tuple-element.82), channel_id=1, source_target_pairs={{4,0},{8,4},{12,8},{16,12},{20,16},{24,20},{28,24},{32,28},{36,32}... | collective-permute-start | bytes 1966088 | tf_op jit(solution)/shard_map/ppermute | solution.py:18
  31.5 4.6 copy-start.3
  140.9 7.1 copy-start.5
  140.9 55.8 %all-to-all-start = ((bf16[80,8,2048]{0,1,2:T(8,128)(2,1)}), bf16[80,8,2048]{0,1,2:T(8,128)(2,1)}, u32[]{:S(2)}, u32[]{:S(2)}) async-start(bf16[80,8,2048]{0,1,2:T(8,128)(2,1)} %copy.24), calls=%async_computation | async-start | bytes 8388608 | tf_op jit(solution)/shard_map/all_to_all | solution.py:73
  148.0 588.0 %all-reduce.24.cloned.1.call-start = ((), (), s32[]{:S(2)}) async-start(), calls=%async_computation.1 | async-start | bytes 36864000
  204.6 1.5 copy-start.2
  514.4 223.2 %copy-start.1 = (s32[8,2048]{1,0:T(8,128)S(1)}, s32[8,2048]{1,0:T(8,128)}, u32[]{:S(2)}) copy-start(s32[8,2048]{1,0:T(8,128)} %param.14) | copy-start | bytes 196612
Sparse Core Ops, SparseCore 0:
  514.6 221.3 all-reduce.23
where the time goes:
time: 748 us; the launch traced here: 744 us
  waiting for transfers between devices  273 us (36%)
  other arithmetic  170 us (23%)
  local copies, waits for them, and re-layouts  151 us (20%)
  loops' own time  124 us (17%)
  between operations  13.5 us (2%)
  starting transfers between devices  12.4 us (2%)
    unnamed x2, waiting for transfers between devices  222 us
    another operation x1, loops' own time, lag_sums(): lagged = lax.map(one_group, lag_groups)  124 us
    reduce_sum x8, other arithmetic, one_group(): jnp.sum(series.astype(jnp.float32) * window.astype(jnp.float32), axis=0)  73.2 us
    slice x6, local copies, waits for them, and re-layouts, shift_columns(): return jnp.concatenate([zero_pad, values[..., :offset]], axis=-1)  59 us
    convert_element_type x1, other arithmetic, smooth_rows(): return running.astype(jnp.bfloat16)  50.3 us
    all_to_all x1, waiting for transfers between devices, per_device(): lax.all_to_all(smoothed, 'tm', split_axis=2, concat_axis=0, tiled=True)  47.4 us
    scatter-add x1, other arithmetic, per_device(): bin_table.at[:, labels_here.reshape(-1)].add(lagged.reshape(lag_count, -1))  36.8 us
    scatter-add x1, local copies, waits for them, and re-layouts, per_device(): bin_table.at[:, labels_here.reshape(-1)].add(lagged.reshape(lag_count, -1))  27.3 us
  transfers between devices with their start and end apart: 4, of which 3 were waited for; matrix products, arithmetic and copies ran while one was open for 2% of the time, Pallas kernels for 0%

commit v1 on v0

v1 whole, which is shorter than its diff:
```python
import functools

import jax
import jax.numpy as jnp
import numpy as np
from jax import lax
from jax.experimental import pallas as pl
from jax.experimental.pallas import tpu as pltpu
from jax.sharding import PartitionSpec as P

F32 = jnp.float32
BF16 = jnp.bfloat16
MESH = pl.DeviceIdType.MESH
VMEM = pltpu.MemorySpace.VMEM
SMEM = pltpu.MemorySpace.SMEM

ROWS8 = 8
W = 2048
FB = 80
TM = 4
QUARTER = W // TM
FRAMES = FB * TM
LAGS = 64
HALF = 36000
BW = 1152
NB = 64
CAP = 128
NDFT = 400
FPAD = 208
MROWS = 80


def dft_tables():
    t = np.arange(FRAMES)
    f = np.arange(NDFT // 2 + 1)
    angle = 2 * np.pi * ((f[:, None] * t[None, :]) % NDFT) / NDFT
    forward = np.zeros((2 * FPAD, FRAMES), np.float64)
    forward[: f.size] = np.cos(angle)
    forward[FPAD : FPAD + f.size] = np.sin(angle)
    k = np.arange(80)
    back = np.zeros((80, FPAD), np.float64)
    fold = np.full(f.size, 2.0)
    fold[0] = fold[-1] = 1.0
    back[:, : f.size] = np.cos(2 * np.pi * ((k[:, None] * f[None, :]) % NDFT) / NDFT) * fold / NDFT

    def split(a):
        hi = a.astype(jnp.bfloat16)
        lo = (a - hi.astype(np.float64)).astype(jnp.bfloat16)
        return hi, lo

    return (*split(forward), *split(back))


def smooth_kernel(taps, before, here, after, out, wp):
    wp[0:2] = before[...]
    wp[2:10] = here[...]
    wp[10:12] = after[...]
    lane = lax.broadcasted_iota(jnp.int32, (16, 128), 1)
    chunks = W // 128

    def one(step, carry):
        fb = step // ROWS8
        i = step % ROWS8
        frames = pl.ds(pl.multiple_of(fb * 16, 16), 16)
        rolled = []
        for c in range(chunks):
            rows = [wp[i + a, frames, c * 128 : (c + 1) * 128].astype(F32) for a in range(5)]
            part = []
            for b in range(5):
                acc = rows[0] * taps[0, b]
                for a in range(1, 5):
                    acc = acc + rows[a] * taps[a, b]
                part.append(acc)
            rolled.append(
                (
                    pltpu.roll(part[0], 2, 1),
                    pltpu.roll(part[1], 1, 1),
                    part[2],
                    pltpu.roll(part[3], 127, 1),
                    pltpu.roll(part[4], 126, 1),
                )
            )
            if c >= 1:
                finish(out, i, frames, c - 1, rolled)
        finish(out, i, frames, chunks - 1, rolled)
        return carry

    def finish(out, i, frames, c, rolled):
        zero = jnp.zeros((16, 128), F32)
        left = rolled[c - 1] if c > 0 else (zero,) * 5
        right = rolled[c + 1] if c + 1 < chunks else (zero,) * 5
        mine = rolled[c]
        total = mine[2]
        total = total + jnp.where(lane >= 2, mine[0], left[0])
        total = total + jnp.where(lane >= 1, mine[1], left[1])
        total = total + jnp.where(lane < 127, mine[3], right[3])
        total = total + jnp.where(lane < 126, mine[4], right[4])
        out[i, frames, c * 128 : (c + 1) * 128] = total.astype(BF16)

    lax.fori_loop(0, (FB // 16) * ROWS8, one, 0)


def smooth(taps, before, here, after):
    return pl.pallas_call(
        smooth_kernel,
        out_shape=jax.ShapeDtypeStruct((ROWS8, FB, W), BF16),
        in_specs=[pl.BlockSpec(memory_space=SMEM)] + [pl.BlockSpec(memory_space=VMEM)] * 3,
        out_specs=pl.BlockSpec(memory_space=VMEM),
        scratch_shapes=[pltpu.VMEM((ROWS8 + 4, FB, W), BF16)],
        compiler_params=pltpu.CompilerParams(vmem_limit_bytes=40 << 20),
        name="smooth",
    )(taps, before, here, after)


def bucket_of(label):
    half = label >= HALF
    inside = jnp.where(half, label - HALF, label)
    quotient = lax.shift_right_logical(lax.shift_right_logical(inside, 7) * 57, 9)
    bucket = jnp.where(half, quotient + 32, quotient)
    return bucket, inside - quotient * BW


def slot_kernel(step_ref, labels, slots, high, low, rounds):
    tm = lax.axis_index("tm")
    cols = pl.ds(pl.multiple_of(tm * QUARTER, QUARTER), QUARTER)
    upper = (
        lax.broadcasted_iota(jnp.int32, (QUARTER, QUARTER), 0)
        <= lax.broadcasted_iota(jnp.int32, (QUARTER, QUARTER), 1)
    ).astype(F32).astype(BF16)
    which = lax.broadcasted_iota(jnp.int32, (NB, QUARTER), 0)
    carry = jnp.zeros((NB, 1), F32)
    first = step_ref[0, 0] * CAP
    for i in range(ROWS8):
        label = labels[i : i + 1, cols]
        bucket, local = bucket_of(label)
        hot = (which == bucket).astype(F32)
        count = jnp.dot(hot.astype(BF16), upper, preferred_element_type=F32) + carry
        rank = jnp.sum(hot * count, axis=0, keepdims=True).astype(jnp.int32) - 1 - first
        inside = (rank >= 0) & (rank < CAP)
        slots[i : i + 1, :] = jnp.where(inside, bucket * CAP + rank, NB * CAP)
        top = lax.shift_right_logical(local, 7)
        high[i : i + 1, :] = top.astype(F32)
        low[i : i + 1, :] = (local - top * 128).astype(F32)
        carry = count[:, QUARTER - 1 : QUARTER]
    most = jnp.max(carry, axis=0, keepdims=True)
    needed = lax.shift_right_logical(most.astype(jnp.int32) + (CAP - 1), 7).astype(F32)
    rounds[...] = jnp.broadcast_to(needed, (8, QUARTER))


def slot_tables(step, labels):
    small = jax.ShapeDtypeStruct((ROWS8, QUARTER), F32)
    return pl.pallas_call(
        slot_kernel,
        out_shape=(jax.ShapeDtypeStruct((ROWS8, QUARTER), jnp.int32), small, small, small),
        in_specs=[pl.BlockSpec(memory_space=SMEM), pl.BlockSpec(memory_space=VMEM)],
        out_specs=(pl.BlockSpec(memory_space=VMEM),) * 4,
        name="slots",
    )(step, labels)


def lag_kernel(slots, series, high, low, rounds, lag_rows, fhi, flo, bhi, blo, out, src, dst):
    lag = lag_rows[...]
    pick = (lag[:, :80] == lax.broadcasted_iota(jnp.int32, (LAGS, 80), 1)).astype(F32).astype(BF16)
    chi = jnp.dot(pick, bhi[...], preferred_element_type=F32).astype(BF16)
    clo = jnp.dot(pick, blo[...], preferred_element_type=F32).astype(BF16)
    scale = 1.0 / (FRAMES - lag[:, :1].astype(F32))
    sub = lax.broadcasted_iota(jnp.int32, (8, QUARTER), 0)

    def clear(j, carry):
        dst[pl.ds(pl.multiple_of(j * 128, 128), 128), :] = jnp.zeros((128, 128), F32)
        return carry

    lax.fori_loop(0, NB, clear, 0)

    def row(i, carry):
        s = series[i]
        x = jnp.dot(fhi[...], s, preferred_element_type=F32)
        x = x + jnp.dot(flo[...], s, preferred_element_type=F32)
        power = x[:FPAD] * x[:FPAD] + x[FPAD:] * x[FPAD:]
        phi = power.astype(BF16)
        plo = (power - phi.astype(F32)).astype(BF16)
        r = jnp.dot(chi, phi, preferred_element_type=F32)
        r = r + jnp.dot(chi, plo, preferred_element_type=F32)
        r = r + jnp.dot(clo, phi, preferred_element_type=F32)
        r = r * scale
        mine = pl.ds(i, 1)
        extra = jnp.where(
            sub == 0,
            high[mine, :],
            jnp.where(sub == 1, low[mine, :], jnp.where(sub == 2, rounds[mine, :], 0.0)),
        )
        full = jnp.concatenate([r, extra, jnp.zeros((56, QUARTER), F32)], axis=0)
        src[pl.ds(pl.multiple_of(i * QUARTER, QUARTER), QUARTER), :] = full.T
        return carry

    lax.fori_loop(0, ROWS8, row, 0)

    per = 16

    def move(g, carry):
        i = g // (QUARTER // per)
        c = (g % (QUARTER // per)) * per
        base = pl.multiple_of(g * per, per)
        for u in range(per):
            to = slots[i, c + u]
            dst[pl.ds(to, 1), :] = src[pl.ds(base + u, 1), :]
        return carry

    lax.fori_loop(0, ROWS8 * QUARTER // per, move, 0)

    def turn(j, carry):
        block = dst[pl.ds(pl.multiple_of(j * 128, 128), 128), :].T
        out[j] = block[:MROWS].astype(BF16)
        return carry

    lax.fori_loop(0, NB, turn, 0)


def lag_messages(slots, series, high, low, rounds, lag_rows, tables):
    return pl.pallas_call(
        lag_kernel,
        out_shape=jax.ShapeDtypeStruct((NB, MROWS, CAP), BF16),
        in_specs=[pl.BlockSpec(memory_space=SMEM)] + [pl.BlockSpec(memory_space=VMEM)] * 9,
        out_specs=pl.BlockSpec(memory_space=VMEM),
        scratch_shapes=[
            pltpu.VMEM((ROWS8 * QUARTER, 128), F32),
            pltpu.VMEM((NB * CAP + 8, 128), F32),
        ],
        compiler_params=pltpu.CompilerParams(vmem_limit_bytes=40 << 20),
        name="lags",
    )(slots, series, high, low, rounds, lag_rows, *tables)


def position():
    rows = lax.axis_index("rows")
    tm = lax.axis_index("tm")
    y = rows // 8
    z = (tm // 2) * 2 + (rows // 4) % 2
    x = rows % 4
    return x, y, z, tm % 2


def at_offset(i, sign):
    x, y, z, _ = position()
    x = (x + sign * (i % 4) + 4) % 4
    y = (y + sign * ((i // 4) % 4) + 4) % 4
    z = (z + sign * (i // 16) + 4) % 4
    rows = y * 8 + (z % 2) * 4 + x
    return rows, z // 2


def bin_kernel(msgs, out, most, recv, acc, tops, fin, got, send_sem, recv_sem, fsend, frecv):
    rows_me = lax.axis_index("rows")
    tm_me = lax.axis_index("tm")
    core = tm_me % 2
    chip = rows_me * 2 + tm_me // 2

    barrier = pltpu.get_barrier_semaphore()

    def greet(i, carry):
        rows, zh = at_offset(i, 1)
        for c in range(2):

            @pl.when((i != 0) | (c != core))
            def _():
                pl.semaphore_signal(barrier, inc=1, device_id=(rows, zh * 2 + c), device_id_type=MESH)

        return carry

    lax.fori_loop(0, NB, greet, 0)
    pl.semaphore_wait(barrier, 2 * NB - 1)

    def route(i, sign):
        rows, zh = at_offset(i, sign)
        there = rows * 2 + zh
        return pltpu.make_async_remote_copy(
            src_ref=msgs.at[there],
            dst_ref=recv.at[i],
            send_sem=send_sem.at[i],
            recv_sem=recv_sem.at[i],
            device_id=(rows, zh * 2 + core),
            device_id_type=MESH,
        )

    def send(i, carry):
        route(i, 1).start()
        return carry

    lax.fori_loop(1, NB, send, 0)

    acc[...] = jnp.zeros_like(acc)
    tops[...] = jnp.zeros_like(tops)
    row_id = lax.broadcasted_iota(jnp.int32, (128, 2 * CAP), 0).astype(F32)

    def add(first, second):
        both = jnp.concatenate([first, second], axis=1)
        values = both[:LAGS]
        extra = both[LAGS : LAGS + 16].astype(F32)
        high, low = extra[0:1], extra[1:2]
        tops[...] = jnp.maximum(tops[...], extra[2:3])
        for h in range(BW // 128):
            key = jnp.where(high == h, low, -1.0)
            hot = jnp.where(row_id == key, 1.0, 0.0).astype(BF16)
            acc[:, h * 128 : (h + 1) * 128] += lax.dot_general(
                values, hot, (((1,), (1,)), ((), ())), preferred_element_type=F32
            )

    route(1, 1).wait_recv()
    add(msgs[chip], recv[1])

    def pair(g, carry):
        i = 2 * g
        route(i, 1).wait_recv()
        route(i + 1, 1).wait_recv()
        add(recv[i], recv[i + 1])
        return carry

    lax.fori_loop(1, NB // 2, pair, 0)

    for h in range(BW // 128):
        fin[:, h, :] = acc[:, h * 128 : (h + 1) * 128]
    peak = jnp.max(tops[...], axis=1, keepdims=True)
    fin[:, BW // 128, :] = jnp.broadcast_to(peak, (LAGS, 128))

    half = chip // 32
    place = core * 32 + chip % 32

    def owner(i):
        rows, zh = at_offset(i, 1)
        there = rows * 2 + zh
        return pltpu.make_async_remote_copy(
            src_ref=fin.at[there],
            dst_ref=got.at[place],
            send_sem=fsend.at[i],
            recv_sem=frecv.at[place],
            device_id=(rows, zh * 2 + half),
            device_id_type=MESH,
        )

    def hand(i, carry):
        owner(i).start()
        return carry

    lax.fori_loop(1, NB, hand, 0)

    own = pltpu.make_async_copy(fin.at[chip], got.at[place], frecv.at[place])

    @pl.when(half == core)
    def _():
        own.start()

    @pl.when(half != core)
    def _():
        owner(0).start()

    def arrived(n, carry):
        pltpu.make_async_copy(got.at[n], got.at[n], frecv.at[n]).wait()
        return carry

    lax.fori_loop(0, NB, arrived, 0)

    top = jnp.zeros((1, 128), F32)
    for j in range(32):
        out[9 * j : 9 * j + 9, :] = got[j, 0:9, :] + got[32 + j, 0:9, :]
        top = jnp.maximum(top, jnp.maximum(got[j, 9:10, :], got[32 + j, 9:10, :]))
    most[...] = jnp.broadcast_to(top, (8, 128))

    def drain(i, carry):
        route(i, 1).wait_send()
        owner(i).wait_send()
        return carry

    lax.fori_loop(1, NB, drain, 0)

    @pl.when(half != core)
    def _():
        owner(0).wait_send()


def bin_sums(msgs):
    return pl.pallas_call(
        bin_kernel,
        out_shape=(
            jax.ShapeDtypeStruct((32 * BW // 128, 128), F32),
            jax.ShapeDtypeStruct((8, 128), F32),
        ),
        in_specs=[pl.BlockSpec(memory_space=VMEM)],
        out_specs=(pl.BlockSpec(memory_space=VMEM),) * 2,
        scratch_shapes=[
            pltpu.VMEM((NB, MROWS, CAP), BF16),
            pltpu.VMEM((LAGS, BW), F32),
            pltpu.VMEM((1, 2 * CAP), F32),
            pltpu.VMEM((LAGS, BW // 128 + 1, 128), F32),
            pltpu.VMEM((NB, BW // 128 + 1, 128), F32),
            pltpu.SemaphoreType.DMA((NB,)),
            pltpu.SemaphoreType.DMA((NB,)),
            pltpu.SemaphoreType.DMA((NB,)),
            pltpu.SemaphoreType.DMA((NB,)),
        ],
        compiler_params=pltpu.CompilerParams(
            collective_id=1, has_side_effects=True, vmem_limit_bytes=40 << 20
        ),
        name="bins",
    )(msgs)


def per_device(
    raw_frames, dark_frame, flat_field, pixel_gain, smoothing_kernel, bin_labels, lag_list
):
    tables = [jnp.asarray(a) for a in dft_tables()]
    weighted = ((raw_frames.astype(F32) - dark_frame) * flat_field * pixel_gain).astype(BF16)
    weighted = jnp.transpose(weighted, (1, 0, 2))
    peers = lax.axis_size("rows")
    up = [(i, i + 1) for i in range(peers - 1)]
    down = [(j, i) for i, j in up]
    before = lax.ppermute(weighted[ROWS8 - 2 :], "rows", up)
    after = lax.ppermute(weighted[:2], "rows", down)
    smoothed = smooth(smoothing_kernel, before, weighted, after)
    series = lax.all_to_all(smoothed, "tm", split_axis=2, concat_axis=1, tiled=True)
    lag_rows = jnp.broadcast_to(lag_list[:, None], (LAGS, 128))

    def one_round(step):
        slots, high, low, rounds = slot_tables(step.reshape(1, 1), bin_labels)
        msgs = lag_messages(slots, series, high, low, rounds, lag_rows, tables)
        return bin_sums(msgs)

    sums, most = one_round(jnp.int32(0))
    needed = most[0, 0].astype(jnp.int32)

    def more(state):
        return state[0] < needed

    def again(state):
        step, total = state
        extra, _ = one_round(step)
        return step + 1, total + extra

    _, sums = lax.while_loop(more, again, (jnp.int32(1), sums))
    return sums.reshape(-1)[:HALF]


def solution(mesh):
    return jax.shard_map(
        per_device,
        mesh=mesh,
        in_specs=(
            P("tm", "rows", None),
            P("rows", None),
            P("rows", None),
            P("rows", None),
            P(),
            P("rows", None),
            P(),
        ),
        out_specs=P(("rows", "tm")),
        check_vma=False,
    )
```

time: 748 us -> 182 us (0.24)
  waiting for transfers between devices: 273 us -> 63.2 us
  other arithmetic: 170 us -> 3.53 us
  local copies, waits for them, and re-layouts: 151 us -> 12 us
  loops' own time: 124 us -> 0.01 us
  Pallas kernels: 0 us -> 88.6 us
  between operations: 13.5 us -> 0.86 us
    unnamed x2 -> x0, waiting for transfers between devices: 222 us -> none
    another operation x1, loops' own time: 124 us -> 0.01 us  [per_device(): _, sums = lax.while_loop(more, again, (jnp.int32(1), sums))]
    pallas_call x0 -> x4, Pallas kernels: none -> 88.6 us  [the longest x1 47 us: bin_sums(): pl.pallas_call(bin_kernel, out_shape=(jax.ShapeDtypeStruct((32 * BW // 12...]
    reduce_sum x8 -> x0, other arithmetic: 73.2 us -> none  [one_group(): jnp.sum(series.astype(jnp.float32) * window.astype(jnp.float32), axis=0)]
    slice x17 -> x2, local copies, waits for them, and re-layouts: 66 us -> 0.65 us  [the longest x1 0.51 us: per_device(): needed = most[0, 0].astype(jnp.int32)]
    convert_element_type x3 -> x0, other arithmetic: 58.4 us -> none  [the longest x1 50.3 us: smooth_rows(): return running.astype(jnp.bfloat16)]
    scatter-add x1 -> x0, other arithmetic: 36.8 us -> none  [per_device(): bin_table.at[:, labels_here.reshape(-1)].add(lagged.reshape(lag_count, -1))]
    scatter-add x1 -> x0, local copies, waits for them, and re-layouts: 27.3 us -> none  [per_device(): bin_table.at[:, labels_here.reshape(-1)].add(lagged.reshape(lag_count, -1))]
  transfers between devices with their start and end apart: 4 -> 3, of which waited for: 3 -> 3; matrix products, arithmetic and copies ran while one was open for 2% -> 0% of each run, Pallas kernels for 0% -> 1%
where the time goes in v1:
time: 182 us; the launch traced here: 181 us
  Pallas kernels  88.6 us (49%)
  waiting for transfers between devices  63.2 us (35%)
  starting transfers between devices  12.4 us (7%)
  local copies, waits for them, and re-layouts  12 us (7%)
  other arithmetic  3.53 us (2%)
    all_to_all x1, waiting for transfers between devices, per_device(): lax.all_to_all(smoothed, 'tm', split_axis=2, concat_axis=1, tiled=True)  47.3 us
    pallas_call x1, Pallas kernels, bin_sums(): pl.pallas_call(bin_kernel, out_shape=(jax.ShapeDtypeStruct((32 * BW // 12...  47 us
    pallas_call x1, Pallas kernels, lag_messages(): pl.pallas_call(lag_kernel, out_shape=jax.ShapeDtypeStruct((NB, MROWS, CAP...  27.1 us
    pallas_call x1, Pallas kernels, smooth(): pl.pallas_call(smooth_kernel, out_shape=jax.ShapeDtypeStruct((ROWS8, FB,...  13 us
    ppermute x1, waiting for transfers between devices, per_device(): before = lax.ppermute(weighted[ROWS8 - 2:], 'rows', up)  12.1 us
    all_to_all x1, starting transfers between devices, per_device(): lax.all_to_all(smoothed, 'tm', split_axis=2, concat_axis=1, tiled=True)  7.08 us
    all_to_all x1, local copies, waits for them, and re-layouts, per_device(): lax.all_to_all(smoothed, 'tm', split_axis=2, concat_axis=1, tiled=True)  5.82 us
    pallas_call x1, local copies, waits for them, and re-layouts, smooth(): pl.pallas_call(smooth_kernel, out_shape=jax.ShapeDtypeStruct((ROWS8, FB,...  4.75 us
  transfers between devices with their start and end apart: 3, of which 3 were waited for; matrix products, arithmetic and copies ran while one was open for 0% of the time, Pallas kernels for 1%

profile of v1, /device:TPU:1, one launch (start us, length us, event | category | flops | bytes accessed | tf_op | source)
XLA Modules:
  0.0 180.6 jit_solution(9586340706587443464)
XLA Ops:
  0.0 3.5 %fusion.2.here = bf16[8,80,2048]{2,1,0:T(8,128)(2,1)S(1)} fusion(bf16[80,8,2048]{2,1,0:T(8,128)(2,1)} %param.13, f32[8,2048]{1,0:T(8,128)} %param.16, f32[8,2048]{1,0:T(8,128)} %param.15, f32[8,2048]{1,0:T(8,128)} %param.14), kind=kLoop, calls=%fused_computation.2 | loop fusion | flops 6553600 | bytes 5439488 | tf_op jit(solution)/shard_map/transpose | solution.py:412
  3.5 0.0 copy-start.12
  3.5 0.1 fusion.3
  3.7 4.0 %collective-permute-start = (bf16[2,80,2048]{2,1,0:T(8,128)(2,1)S(1)}, bf16[2,80,2048]{2,1,0:T(8,128)(2,1)S(1)}, u32[]{:S(2)}, u32[]{:S(2)}) collective-permute-start(bf16[2,80,2048]{2,1,0:T(8,128)(2,1)S(1)} %get-tuple-element.148), channel_id=1, source_target_pairs={{0,4},{4,8},{8,12},{12,16},{16,20},{20,24},{24,28},{28,32},{32,36}... | collective-permute-start | bytes 1966088 | tf_op jit(solution)/shard_map/ppermute | solution.py:416
  7.7 1.3 collective-permute-start.1
  9.0 12.1 %collective-permute-done.before = bf16[2,80,2048]{2,1,0:T(8,128)(2,1)S(1)} collective-permute-done((bf16[2,80,2048]{2,1,0:T(8,128)(2,1)S(1)}, bf16[2,80,2048]{2,1,0:T(8,128)(2,1)S(1)}, u32[]{:S(2)}, u32[]{:S(2)}) %collective-permute-start) | collective-permute-done | bytes 655392 | tf_op jit(solution)/shard_map/ppermute | solution.py:416
  21.0 3.9 %collective-permute-done.1.after = bf16[2,80,2048]{2,1,0:T(8,128)(2,1)S(1)} collective-permute-done((bf16[2,80,2048]{2,1,0:T(8,128)(2,1)S(1)}, bf16[2,80,2048]{2,1,0:T(8,128)(2,1)S(1)}, u32[]{:S(2)}, u32[]{:S(2)}) %collective-permute-start.1) | collective-permute-done | bytes 655392 | tf_op jit(solution)/shard_map/ppermute | solution.py:417
  24.9 0.0 copy-done.12
  24.9 13.0 %smooth.1 = bf16[8,80,2048]{2,1,0:T(8,128)(2,1)S(1)} custom-call(f32[5,5]{1,0:T(8,128)S(1)} %copy-done.12, bf16[2,80,2048]{2,1,0:T(8,128)(2,1)S(1)} %collective-permute-done.before, bf16[8,80,2048]{2,1,0:T(8,128)(2,1)S(1)} %fusion.2.here, bf16[2,80,2048]{2,1,0:T(8,128)(2,1)S(1)} %collective-permute-done.1.after), custom_call_target="tpu_custom_call" | custom-call | tf_op jit(solution)/shard_map/smooth/pallas_call | solution.py:104
  38.0 4.7 %copy.15 = bf16[8,80,2048]{1,0,2:T(8,128)(2,1)} copy(bf16[8,80,2048]{2,1,0:T(8,128)(2,1)S(1)} %smooth.1) | data formatting | bytes 5242880 | tf_op jit(solution)/shard_map/smooth/pallas_call | solution.py:104
  42.7 0.0 copy-start.13
  42.7 7.1 %all-to-all-start = ((bf16[8,80,2048]{1,0,2:T(8,128)(2,1)}), bf16[8,80,2048]{1,0,2:T(8,128)(2,1)}, u32[]{:S(2)}, u32[]{:S(2)}) async-start(bf16[8,80,2048]{1,0,2:T(8,128)(2,1)} %copy.15), calls=%async_computation | async-start | bytes 8388608 | tf_op jit(solution)/shard_map/all_to_all | solution.py:419
  49.8 0.0 copy-done.13
  49.8 1.5 slots.2
  51.3 47.3 %all-to-all-done = bf16[8,80,2048]{1,0,2:T(8,128)(2,1)} async-done(((bf16[8,80,2048]{1,0,2:T(8,128)(2,1)}), bf16[8,80,2048]{1,0,2:T(8,128)(2,1)}, u32[]{:S(2)}, u32[]{:S(2)}) %all-to-all-start) | async-done | bytes 2621472 | tf_op jit(solution)/shard_map/all_to_all | solution.py:419
  98.5 0.0 copy-start.16
  98.5 0.0 copy-start.4
  98.5 0.0 copy-start.5
  98.5 0.0 copy-start.6
  98.5 0.0 copy-start.7
  98.6 0.0 copy-start.8
  98.6 0.0 copy-start.9
  98.6 0.0 copy-start.10
  98.6 0.0 copy-start.11
  98.6 5.8 %copy.16 = bf16[8,80,4,512]{3,1,2,0:T(8,128)(2,1)S(1)} copy(bf16[8,80,4,512]{1,0,3,2:T(8,128)(2,1)} %bitcast.1) | data formatting | bytes 5242880 | tf_op jit(solution)/shard_map/all_to_all | solution.py:419
  104.4 0.0 copy-done.16
  104.4 0.1 broadcast_in_dim.2.lag_rows
  104.5 0.0 copy-done.4
  104.5 0.0 copy-done.5
  104.5 0.0 copy-done.6
  104.5 0.0 copy-done.7
  104.5 0.0 copy-done.8
  104.6 0.0 copy-done.9
  104.6 0.0 copy-done.10
  104.6 0.0 copy-done.11
  104.6 0.0 copy-start.14
  104.6 0.0 copy-start.15
  104.6 27.1 %lags.2.msgs = bf16[64,80,128]{2,1,0:T(8,128)(2,1)S(1)} custom-call(s32[8,512]{1,0:T(8,128)S(1)} %copy-done.8, bf16[8,320,512]{2,1,0:T(8,128)(2,1)S(1)} %bitcast.12, f32[8,512]{1,0:T(8,128)S(1)} %copy-done.9, f32[8,512]{1,0:T(8,128)S(1)} %copy-done.10, f32[8,512]{1,0:T(8,128)S(1)} %copy-done.11, s32[64,128]{1,0:T(8,128)S(1)} %broadcast_in_dim.2.lag_rows, ...), custom_call_target="tpu_custom_call" | custom-call | tf_op jit(solution)/shard_map/lags/pallas_call | solution.py:220
  131.7 47.0 %bins.2 = (f32[288,128]{1,0:T(8,128)S(1)}, f32[8,128]{1,0:T(8,128)S(1)}) custom-call(bf16[64,80,128]{2,1,0:T(8,128)(2,1)S(1)} %lags.2.msgs), custom_call_target="tpu_custom_call" | custom-call | tf_op jit(solution)/shard_map/bins/pallas_call | solution.py:381
  178.7 0.5 slice.14
  179.9 0.0 copy-done.14
  179.9 0.0 copy-done.15
  179.9 0.7 copy.25
  (1 shorter events, 0.0 us)
Async XLA Ops:
  3.5 21.4 %copy-start.12 = (f32[5,5]{1,0:T(8,128)S(1)}, f32[5,5]{1,0:T(8,128)}, u32[]{:S(2)}) copy-start(f32[5,5]{1,0:T(8,128)} %taps.1) | copy-start | bytes 304
  3.7 17.3 %collective-permute-start = (bf16[2,80,2048]{2,1,0:T(8,128)(2,1)S(1)}, bf16[2,80,2048]{2,1,0:T(8,128)(2,1)S(1)}, u32[]{:S(2)}, u32[]{:S(2)}) collective-permute-start(bf16[2,80,2048]{2,1,0:T(8,128)(2,1)S(1)} %get-tuple-element.148), channel_id=1, source_target_pairs={{0,4},{4,8},{8,12},{12,16},{16,20},{20,24},{24,28},{28,32},{32,36}... | collective-permute-start | bytes 1966088 | tf_op jit(solution)/shard_map/ppermute | solution.py:416
  7.7 17.2 %collective-permute-start.1 = (bf16[2,80,2048]{2,1,0:T(8,128)(2,1)S(1)}, bf16[2,80,2048]{2,1,0:T(8,128)(2,1)S(1)}, u32[]{:S(2)}, u32[]{:S(2)}) collective-permute-start(bf16[2,80,2048]{2,1,0:T(8,128)(2,1)S(1)} %get-tuple-element.147), channel_id=1, source_target_pairs={{4,0},{8,4},{12,8},{16,12},{20,16},{24,20},{28,24},{32,28},{36,32}... | collective-permute-start | bytes 1966088 | tf_op jit(solution)/shard_map/ppermute | solution.py:417
  42.7 7.1 %copy-start.13 = (s32[8,2048]{1,0:T(8,128)S(1)}, s32[8,2048]{1,0:T(8,128)}, u32[]{:S(2)}) copy-start(s32[8,2048]{1,0:T(8,128)} %labels.1) | copy-start | bytes 196612
  42.7 55.8 %all-to-all-start = ((bf16[8,80,2048]{1,0,2:T(8,128)(2,1)}), bf16[8,80,2048]{1,0,2:T(8,128)(2,1)}, u32[]{:S(2)}, u32[]{:S(2)}) async-start(bf16[8,80,2048]{1,0,2:T(8,128)(2,1)} %copy.15), calls=%async_computation | async-start | bytes 8388608 | tf_op jit(solution)/shard_map/all_to_all | solution.py:419
  98.5 5.9 %copy-start.16 = (s32[64]{0:T(128)S(1)}, s32[64]{0:T(128)}, u32[]{:S(2)}) copy-start(s32[64]{0:T(128)} %param.19) | copy-start | bytes 772
  98.5 6.0 %copy-start.4 = (bf16[416,320]{1,0:T(8,128)(2,1)S(1)}, bf16[416,320]{1,0:T(8,128)(2,1)}, u32[]{:S(2)}) copy-start(bf16[416,320]{1,0:T(8,128)(2,1)} %constant.14.clone.fhi) | copy-start | bytes 798724
  98.5 6.0 %copy-start.5 = (bf16[416,320]{1,0:T(8,128)(2,1)S(1)}, bf16[416,320]{1,0:T(8,128)(2,1)}, u32[]{:S(2)}) copy-start(bf16[416,320]{1,0:T(8,128)(2,1)} %constant.15.clone.flo) | copy-start | bytes 798724
  98.5 6.0 %copy-start.6 = (bf16[80,208]{1,0:T(8,128)(2,1)S(1)}, bf16[80,208]{1,0:T(8,128)(2,1)}, u32[]{:S(2)}) copy-start(bf16[80,208]{1,0:T(8,128)(2,1)} %constant.16.clone.bhi) | copy-start | bytes 99844
  98.5 6.0 %copy-start.7 = (bf16[80,208]{1,0:T(8,128)(2,1)S(1)}, bf16[80,208]{1,0:T(8,128)(2,1)}, u32[]{:S(2)}) copy-start(bf16[80,208]{1,0:T(8,128)(2,1)} %constant.17.clone.blo) | copy-start | bytes 99844
  98.6 6.0 %copy-start.8 = (s32[8,512]{1,0:T(8,128)S(1)}, s32[8,512]{1,0:T(8,128)}, u32[]{:S(2)}) copy-start(s32[8,512]{1,0:T(8,128)} %get-tuple-element.69.slots) | copy-start | bytes 49156
  98.6 6.0 %copy-start.9 = (f32[8,512]{1,0:T(8,128)S(1)}, f32[8,512]{1,0:T(8,128)}, u32[]{:S(2)}) copy-start(f32[8,512]{1,0:T(8,128)} %get-tuple-element.70.high) | copy-start | bytes 49156
  98.6 6.0 %copy-start.10 = (f32[8,512]{1,0:T(8,128)S(1)}, f32[8,512]{1,0:T(8,128)}, u32[]{:S(2)}) copy-start(f32[8,512]{1,0:T(8,128)} %get-tuple-element.71.low) | copy-start | bytes 49156
  98.6 6.0 %copy-start.11 = (f32[8,512]{1,0:T(8,128)S(1)}, f32[8,512]{1,0:T(8,128)}, u32[]{:S(2)}) copy-start(f32[8,512]{1,0:T(8,128)} %get-tuple-element.72.rounds) | copy-start | bytes 49156
  104.6 75.3 %copy-start.14 = (bf16[80,208]{1,0:T(8,128)(2,1)S(1)}, bf16[80,208]{1,0:T(8,128)(2,1)}, u32[]{:S(2)}) copy-start(bf16[80,208]{1,0:T(8,128)(2,1)} %constant.16.clone..sunk.3) | copy-start | bytes 99844
  104.6 75.3 %copy-start.15 = (bf16[80,208]{1,0:T(8,128)(2,1)S(1)}, bf16[80,208]{1,0:T(8,128)(2,1)}, u32[]{:S(2)}) copy-start(bf16[80,208]{1,0:T(8,128)(2,1)} %constant.17.clone..sunk.3) | copy-start | bytes 99844

commit v2 on v1

--- a/solution.py
+++ b/solution.py
@@ -51,18 +51,26 @@
     return (*split(forward), *split(back))
 
 
-def smooth_kernel(taps, before, here, after, out, wp):
-    wp[0:2] = before[...]
-    wp[2:10] = here[...]
-    wp[10:12] = after[...]
+def smooth_row(taps, wp, out, i):
     lane = lax.broadcasted_iota(jnp.int32, (16, 128), 1)
+    zero = jnp.zeros((16, 128), F32)
     chunks = W // 128
 
-    def one(step, carry):
-        fb = step // ROWS8
-        i = step % ROWS8
+    def one(fb, carry):
         frames = pl.ds(pl.multiple_of(fb * 16, 16), 16)
         rolled = []
+
+        def finish(c):
+            left = rolled[c - 1] if c > 0 else (zero,) * 5
+            right = rolled[c + 1] if c + 1 < chunks else (zero,) * 5
+            mine = rolled[c]
+            total = mine[2]
+            total = total + jnp.where(lane >= 2, mine[0], left[0])
+            total = total + jnp.where(lane >= 1, mine[1], left[1])
+            total = total + jnp.where(lane < 127, mine[3], right[3])
+            total = total + jnp.where(lane < 126, mine[4], right[4])
+            out[i, frames, c * 128 : (c + 1) * 128] = total.astype(BF16)
+
         for c in range(chunks):
             rows = [wp[i + a, frames, c * 128 : (c + 1) * 128].astype(F32) for a in range(5)]
             part = []
@@ -81,35 +89,11 @@
                 )
             )
             if c >= 1:
-                finish(out, i, frames, c - 1, rolled)
-        finish(out, i, frames, chunks - 1, rolled)
-        return carry
-
-    def finish(out, i, frames, c, rolled):
-        zero = jnp.zeros((16, 128), F32)
-        left = rolled[c - 1] if c > 0 else (zero,) * 5
-        right = rolled[c + 1] if c + 1 < chunks else (zero,) * 5
-        mine = rolled[c]
-        total = mine[2]
-        total = total + jnp.where(lane >= 2, mine[0], left[0])
-        total = total + jnp.where(lane >= 1, mine[1], left[1])
-        total = total + jnp.where(lane < 127, mine[3], right[3])
-        total = total + jnp.where(lane < 126, mine[4], right[4])
-        out[i, frames, c * 128 : (c + 1) * 128] = total.astype(BF16)
-
-    lax.fori_loop(0, (FB // 16) * ROWS8, one, 0)
-
-
-def smooth(taps, before, here, after):
-    return pl.pallas_call(
-        smooth_kernel,
-        out_shape=jax.ShapeDtypeStruct((ROWS8, FB, W), BF16),
-        in_specs=[pl.BlockSpec(memory_space=SMEM)] + [pl.BlockSpec(memory_space=VMEM)] * 3,
-        out_specs=pl.BlockSpec(memory_space=VMEM),
-        scratch_shapes=[pltpu.VMEM((ROWS8 + 4, FB, W), BF16)],
-        compiler_params=pltpu.CompilerParams(vmem_limit_bytes=40 << 20),
-        name="smooth",
-    )(taps, before, here, after)
+                finish(c - 1)
+        finish(chunks - 1)
+        return carry
+
+    lax.fori_loop(0, FB // 16, one, 0)
 
 
 def bucket_of(label):
@@ -120,45 +104,160 @@
     return bucket, inside - quotient * BW
 
 
-def slot_kernel(step_ref, labels, slots, high, low, rounds):
-    tm = lax.axis_index("tm")
-    cols = pl.ds(pl.multiple_of(tm * QUARTER, QUARTER), QUARTER)
+def fill_slots(labels, first, slots, parts=None):
     upper = (
         lax.broadcasted_iota(jnp.int32, (QUARTER, QUARTER), 0)
         <= lax.broadcasted_iota(jnp.int32, (QUARTER, QUARTER), 1)
     ).astype(F32).astype(BF16)
     which = lax.broadcasted_iota(jnp.int32, (NB, QUARTER), 0)
+    sub = lax.broadcasted_iota(jnp.int32, (8, QUARTER), 0)
     carry = jnp.zeros((NB, 1), F32)
-    first = step_ref[0, 0] * CAP
     for i in range(ROWS8):
-        label = labels[i : i + 1, cols]
-        bucket, local = bucket_of(label)
+        bucket, local = bucket_of(labels[i : i + 1, :])
         hot = (which == bucket).astype(F32)
         count = jnp.dot(hot.astype(BF16), upper, preferred_element_type=F32) + carry
         rank = jnp.sum(hot * count, axis=0, keepdims=True).astype(jnp.int32) - 1 - first
         inside = (rank >= 0) & (rank < CAP)
         slots[i : i + 1, :] = jnp.where(inside, bucket * CAP + rank, NB * CAP)
-        top = lax.shift_right_logical(local, 7)
-        high[i : i + 1, :] = top.astype(F32)
-        low[i : i + 1, :] = (local - top * 128).astype(F32)
+        if parts is not None:
+            top = lax.shift_right_logical(local, 7)
+            low = local - top * 128
+            parts[i] = jnp.where(sub == 0, top.astype(F32), jnp.where(sub == 1, low.astype(F32), 0.0))
         carry = count[:, QUARTER - 1 : QUARTER]
     most = jnp.max(carry, axis=0, keepdims=True)
-    needed = lax.shift_right_logical(most.astype(jnp.int32) + (CAP - 1), 7).astype(F32)
-    rounds[...] = jnp.broadcast_to(needed, (8, QUARTER))
-
-
-def slot_tables(step, labels):
-    small = jax.ShapeDtypeStruct((ROWS8, QUARTER), F32)
+    return lax.shift_right_logical(most.astype(jnp.int32) + (CAP - 1), 7).astype(F32)
+
+
+def slot_kernel(step_ref, labels, slots):
+    fill_slots(labels, step_ref[0, 0] * CAP, slots)
+
+
+def later_slots(step, labels):
     return pl.pallas_call(
         slot_kernel,
-        out_shape=(jax.ShapeDtypeStruct((ROWS8, QUARTER), jnp.int32), small, small, small),
+        out_shape=jax.ShapeDtypeStruct((ROWS8, QUARTER), jnp.int32),
         in_specs=[pl.BlockSpec(memory_space=SMEM), pl.BlockSpec(memory_space=VMEM)],
-        out_specs=(pl.BlockSpec(memory_space=VMEM),) * 4,
+        out_specs=pl.BlockSpec(memory_space=VMEM),
         name="slots",
     )(step, labels)
 
 
-def lag_kernel(slots, series, high, low, rounds, lag_rows, fhi, flo, bhi, blo, out, src, dst):
+def front_kernel(
+    taps, raw, dark, flat, gain, all_labels, lag_rows, fhi, flo, bhi, blo,
+    src, slots, labels_out,
+    wp, smoothed, series, labels, parts,
+    hsend, hrecv, zsend, zrecv, lsend, lrecv,
+):
+    rows = lax.axis_index("rows")
+    tm = lax.axis_index("tm")
+    over = rows + 4 - 8 * ((rows // 4) % 2)
+    not_first = (rows + 31) // 32
+    not_last = 1 - (rows + 1) // 32
+
+    barrier = pltpu.get_barrier_semaphore()
+
+    def greet(r, t):
+        pl.semaphore_signal(barrier, inc=1, device_id=(r, t), device_id_type=MESH)
+
+    @pl.when(rows > 0)
+    def _():
+        greet(rows - 1, tm)
+
+    @pl.when(rows < 31)
+    def _():
+        greet(rows + 1, tm)
+
+    for q in range(TM):
+        greet(over, q)
+
+    blocks = FB // 16
+
+    def to_next(q):
+        frames = pl.ds(q * 16, 16)
+        return pltpu.make_async_remote_copy(
+            src_ref=wp.at[8:10, frames], dst_ref=wp.at[0:2, frames],
+            send_sem=hsend.at[0, q], recv_sem=hrecv.at[0, q],
+            device_id=(rows + 1, tm), device_id_type=MESH,
+        )
+
+    def to_previous(q):
+        frames = pl.ds(q * 16, 16)
+        return pltpu.make_async_remote_copy(
+            src_ref=wp.at[2:4, frames], dst_ref=wp.at[10:12, frames],
+            send_sem=hsend.at[1, q], recv_sem=hrecv.at[1, q],
+            device_id=(rows - 1, tm), device_id_type=MESH,
+        )
+
+    label_copy = pltpu.make_async_remote_copy(
+        src_ref=all_labels.at[:, pl.ds(pl.multiple_of(tm * QUARTER, QUARTER), QUARTER)],
+        dst_ref=labels, send_sem=lsend, recv_sem=lrecv,
+        device_id=(over, tm), device_id_type=MESH,
+    )
+
+    @pl.when(rows == 0)
+    def _():
+        wp[0:2] = jnp.zeros((2, FB, W), BF16)
+
+    @pl.when(rows == 31)
+    def _():
+        wp[10:12] = jnp.zeros((2, FB, W), BF16)
+
+    cols = 256
+    for q in range(blocks):
+
+        def weigh(c, carry):
+            at = pl.ds(pl.multiple_of(c * cols, cols), cols)
+            x = raw[q * 16 : (q + 1) * 16, :, at].astype(F32)
+            x = (x - dark[:, at][None]) * flat[:, at][None] * gain[:, at][None]
+            wp[2:10, q * 16 : (q + 1) * 16, at] = jnp.swapaxes(x, 0, 1).astype(BF16)
+            return carry
+
+        lax.fori_loop(0, W // cols, weigh, 0)
+
+        if q == 0:
+            pl.semaphore_wait(barrier, TM + not_first + not_last)
+            label_copy.start()
+
+        @pl.when(rows < 31)
+        def _():
+            to_next(q).start()
+
+        @pl.when(rows > 0)
+        def _():
+            to_previous(q).start()
+
+    def across(i, q):
+        return pltpu.make_async_remote_copy(
+            src_ref=smoothed.at[i, :, q * QUARTER : (q + 1) * QUARTER],
+            dst_ref=series.at[i, pl.ds(pl.multiple_of(tm * FB, FB), FB), :],
+            send_sem=zsend.at[i, q], recv_sem=zrecv.at[i, tm],
+            device_id=(over, q), device_id_type=MESH,
+        )
+
+    def row(n, carry):
+        i = (n + 2) % ROWS8
+
+        @pl.when((n == 4) & (rows < 31))
+        def _():
+            for q in range(blocks):
+                to_previous(q).wait_recv()
+
+        @pl.when((n == 6) & (rows > 0))
+        def _():
+            for q in range(blocks):
+                to_next(q).wait_recv()
+
+        smooth_row(taps, wp, smoothed, i)
+        for q in range(TM):
+            across(i, q).start()
+        return carry
+
+    lax.fori_loop(0, ROWS8, row, 0)
+
+    label_copy.wait_recv()
+    labels_out[...] = labels[...]
+    rounds = fill_slots(labels, 0, slots, parts)
+
     lag = lag_rows[...]
     pick = (lag[:, :80] == lax.broadcasted_iota(jnp.int32, (LAGS, 80), 1)).astype(F32).astype(BF16)
     chi = jnp.dot(pick, bhi[...], preferred_element_type=F32).astype(BF16)
@@ -166,13 +265,12 @@
     scale = 1.0 / (FRAMES - lag[:, :1].astype(F32))
     sub = lax.broadcasted_iota(jnp.int32, (8, QUARTER), 0)
 
-    def clear(j, carry):
-        dst[pl.ds(pl.multiple_of(j * 128, 128), 128), :] = jnp.zeros((128, 128), F32)
-        return carry
-
-    lax.fori_loop(0, NB, clear, 0)
-
-    def row(i, carry):
+    def lags(n, carry):
+        i = (n + 2) % ROWS8
+        for t in range(TM):
+            pltpu.make_async_copy(
+                series.at[i, t * FB : (t + 1) * FB], series.at[i, t * FB : (t + 1) * FB], zrecv.at[i, t]
+            ).wait()
         s = series[i]
         x = jnp.dot(fhi[...], s, preferred_element_type=F32)
         x = x + jnp.dot(flo[...], s, preferred_element_type=F32)
@@ -183,17 +281,68 @@
         r = r + jnp.dot(chi, plo, preferred_element_type=F32)
         r = r + jnp.dot(clo, phi, preferred_element_type=F32)
         r = r * scale
-        mine = pl.ds(i, 1)
-        extra = jnp.where(
-            sub == 0,
-            high[mine, :],
-            jnp.where(sub == 1, low[mine, :], jnp.where(sub == 2, rounds[mine, :], 0.0)),
-        )
+        extra = jnp.where(sub == 2, rounds, parts[i])
         full = jnp.concatenate([r, extra, jnp.zeros((56, QUARTER), F32)], axis=0)
         src[pl.ds(pl.multiple_of(i * QUARTER, QUARTER), QUARTER), :] = full.T
         return carry
 
-    lax.fori_loop(0, ROWS8, row, 0)
+    lax.fori_loop(0, ROWS8, lags, 0)
+
+    def drain(i, carry):
+        for q in range(TM):
+            across(i, q).wait_send()
+        return carry
+
+    lax.fori_loop(0, ROWS8, drain, 0)
+    label_copy.wait_send()
+    for q in range(blocks):
+
+        @pl.when(rows < 31)
+        def _():
+            to_next(q).wait_send()
+
+        @pl.when(rows > 0)
+        def _():
+            to_previous(q).wait_send()
+
+
+def frames_to_lags(taps, raw, dark, flat, gain, labels, lag_rows, tables):
+    dma = pltpu.SemaphoreType.DMA
+    return pl.pallas_call(
+        front_kernel,
+        out_shape=(
+            jax.ShapeDtypeStruct((ROWS8 * QUARTER, 128), F32),
+            jax.ShapeDtypeStruct((ROWS8, QUARTER), jnp.int32),
+            jax.ShapeDtypeStruct((ROWS8, QUARTER), jnp.int32),
+        ),
+        in_specs=[pl.BlockSpec(memory_space=SMEM)] + [pl.BlockSpec(memory_space=VMEM)] * 10,
+        out_specs=(pl.BlockSpec(memory_space=VMEM),) * 3,
+        scratch_shapes=[
+            pltpu.VMEM((ROWS8 + 4, FB, W), BF16),
+            pltpu.VMEM((ROWS8, FB, W), BF16),
+            pltpu.VMEM((ROWS8, FRAMES, QUARTER), BF16),
+            pltpu.VMEM((ROWS8, QUARTER), jnp.int32),
+            pltpu.VMEM((ROWS8, 8, QUARTER), F32),
+            dma((2, FB // 16)),
+            dma((2, FB // 16)),
+            dma((ROWS8, TM)),
+            dma((ROWS8, TM)),
+            dma(()),
+            dma(()),
+        ],
+        compiler_params=pltpu.CompilerParams(
+            collective_id=0, has_side_effects=True, vmem_limit_bytes=48 << 20
+        ),
+        name="front",
+    )(taps, raw, dark, flat, gain, labels, lag_rows, *tables)
+
+
+def place_kernel(slots, src, out, dst):
+    def clear(j, carry):
+        dst[pl.ds(pl.multiple_of(j * 128, 128), 128), :] = jnp.zeros((128, 128), F32)
+        return carry
+
+    lax.fori_loop(0, NB, clear, 0)
 
     per = 16
 
@@ -216,19 +365,16 @@
     lax.fori_loop(0, NB, turn, 0)
 
 
-def lag_messages(slots, series, high, low, rounds, lag_rows, tables):
+def place(slots, src):
     return pl.pallas_call(
-        lag_kernel,
+        place_kernel,
         out_shape=jax.ShapeDtypeStruct((NB, MROWS, CAP), BF16),
-        in_specs=[pl.BlockSpec(memory_space=SMEM)] + [pl.BlockSpec(memory_space=VMEM)] * 9,
+        in_specs=[pl.BlockSpec(memory_space=SMEM), pl.BlockSpec(memory_space=VMEM)],
         out_specs=pl.BlockSpec(memory_space=VMEM),
-        scratch_shapes=[
-            pltpu.VMEM((ROWS8 * QUARTER, 128), F32),
-            pltpu.VMEM((NB * CAP + 8, 128), F32),
-        ],
+        scratch_shapes=[pltpu.VMEM((NB * CAP + 8, 128), F32)],
         compiler_params=pltpu.CompilerParams(vmem_limit_bytes=40 << 20),
-        name="lags",
-    )(slots, series, high, low, rounds, lag_rows, *tables)
+        name="place",
+    )(slots, src)
 
 
 def position():
@@ -408,23 +554,11 @@
     raw_frames, dark_frame, flat_field, pixel_gain, smoothing_kernel, bin_labels, lag_list
 ):
     tables = [jnp.asarray(a) for a in dft_tables()]
-    weighted = ((raw_frames.astype(F32) - dark_frame) * flat_field * pixel_gain).astype(BF16)
-    weighted = jnp.transpose(weighted, (1, 0, 2))
-    peers = lax.axis_size("rows")
-    up = [(i, i + 1) for i in range(peers - 1)]
-    down = [(j, i) for i, j in up]
-    before = lax.ppermute(weighted[ROWS8 - 2 :], "rows", up)
-    after = lax.ppermute(weighted[:2], "rows", down)
-    smoothed = smooth(smoothing_kernel, before, weighted, after)
-    series = lax.all_to_all(smoothed, "tm", split_axis=2, concat_axis=1, tiled=True)
     lag_rows = jnp.broadcast_to(lag_list[:, None], (LAGS, 128))
-
-    def one_round(step):
-        slots, high, low, rounds = slot_tables(step.reshape(1, 1), bin_labels)
-        msgs = lag_messages(slots, series, high, low, rounds, lag_rows, tables)
-        return bin_sums(msgs)
-
-    sums, most = one_round(jnp.int32(0))
+    src, slots, labels = frames_to_lags(
+        smoothing_kernel, raw_frames, dark_frame, flat_field, pixel_gain, bin_labels, lag_rows, tables
+    )
+    sums, most = bin_sums(place(slots, src))
     needed = most[0, 0].astype(jnp.int32)
 
     def more(state):
@@ -432,7 +566,7 @@
 
     def again(state):
         step, total = state
-        extra, _ = one_round(step)
+        extra, _ = bin_sums(place(later_slots(step.reshape(1, 1), labels), src))
         return step + 1, total + extra
 
     _, sums = lax.while_loop(more, again, (jnp.int32(1), sums))

time: 182 us -> 129 us (0.71)
  waiting for transfers between devices: 63.2 us -> 0 us
  Pallas kernels: 88.6 us -> 116 us
  starting transfers between devices: 12.4 us -> 0 us
  other arithmetic: 3.53 us -> 0 us
    all_to_all x1 -> x0, waiting for transfers between devices: 47.3 us -> none  [per_device(): lax.all_to_all(smoothed, 'tm', split_axis=2, concat_axis=1, tiled=True)]
    pallas_call x3 -> x2, Pallas kernels: 41.6 us -> 70.8 us  [the longest x1 51.4 us: frames_to_lags(): pl.pallas_call(front_kernel, out_shape=(jax.ShapeDtypeStruct((ROWS8 * QUA...]
    ppermute x2 -> x0, waiting for transfers between devices: 15.9 us -> none  [the longest x1 12.1 us: per_device(): before = lax.ppermute(weighted[ROWS8 - 2:], 'rows', up)]
    unnamed x27 -> x21, local copies, waits for them, and re-layouts: 0.74 us -> 9.95 us
    all_to_all x1 -> x0, starting transfers between devices: 7.08 us -> none  [per_device(): lax.all_to_all(smoothed, 'tm', split_axis=2, concat_axis=1, tiled=True)]
    all_to_all x1 -> x0, local copies, waits for them, and re-layouts: 5.82 us -> none  [per_device(): lax.all_to_all(smoothed, 'tm', split_axis=2, concat_axis=1, tiled=True)]
    ppermute x2 -> x0, starting transfers between devices: 5.27 us -> none  [the longest x1 3.97 us: per_device(): before = lax.ppermute(weighted[ROWS8 - 2:], 'rows', up)]
    pallas_call x1 -> x0, local copies, waits for them, and re-layouts: 4.75 us -> none  [smooth(): pl.pallas_call(smooth_kernel, out_shape=jax.ShapeDtypeStruct((ROWS8, FB,...]
  transfers between devices with their start and end apart: 3 -> 0, of which waited for: 3 -> 0; matrix products, arithmetic and copies ran while one was open for 0% -> 0% of each run, Pallas kernels for 1% -> 0%
where the time goes in v2:
time: 129 us; the launch traced here: 128 us
  Pallas kernels  116 us (90%)
  local copies, waits for them, and re-layouts  11.2 us (9%)
    pallas_call x1, Pallas kernels, frames_to_lags(): pl.pallas_call(front_kernel, out_shape=(jax.ShapeDtypeStruct((ROWS8 * QUA...  51.4 us
    pallas_call x1, Pallas kernels, bin_sums(): pl.pallas_call(bin_kernel, out_shape=(jax.ShapeDtypeStruct((32 * BW // 12...  45.4 us
    pallas_call x1, Pallas kernels, place(): pl.pallas_call(place_kernel, out_shape=jax.ShapeDtypeStruct((NB, MROWS, C...  19.4 us
    unnamed x21, local copies, waits for them, and re-layouts  9.95 us

profile of v2, /device:TPU:1, one launch (start us, length us, event | category | flops | bytes accessed | tf_op | source)
XLA Modules:
  0.0 128.0 jit_solution(14011474381908861233)
XLA Ops:
  0.0 0.7 broadcast_in_dim.2.lag_rows
  0.7 0.0 copy-start
  0.7 1.7 %copy-done = bf16[80,8,2048]{2,1,0:T(8,128)(2,1)S(1)} copy-done((bf16[80,8,2048]{2,1,0:T(8,128)(2,1)S(1)}, bf16[80,8,2048]{2,1,0:T(8,128)(2,1)}, u32[]{:S(2)}) %copy-start) | copy-done | bytes 2621464
  2.5 0.0 copy-start.2
  2.5 1.0 copy-done.2
  3.4 0.0 copy-start.3
  3.4 1.0 copy-done.3
  4.4 0.0 copy-start.4
  4.4 0.8 copy-done.4
  5.3 0.0 copy-start.5
  5.3 0.8 copy-done.5
  6.1 0.0 copy-start.6
  6.1 0.8 copy-done.6
  6.9 0.0 copy-start.7
  6.9 0.8 copy-done.7
  7.8 0.0 copy-start.8
  7.8 0.8 copy-done.8
  8.6 0.0 copy-start.9
  8.6 0.8 copy-done.9
  9.3 0.0 copy-start.10
  9.3 0.7 copy-done.10
  10.0 51.4 %front.1 = (f32[4096,128]{1,0:T(8,128)S(1)}, s32[8,512]{1,0:T(8,128)S(1)}, s32[8,512]{1,0:T(8,128)S(1)}) custom-call(f32[5,5]{1,0:T(8,128)S(1)} %copy-done.10, bf16[80,8,2048]{2,1,0:T(8,128)(2,1)S(1)} %copy-done, f32[8,2048]{1,0:T(8,128)S(1)} %copy-done.4, f32[8,2048]{1,0:T(8,128)S(1)} %copy-done.5, f32[8,2048]{1,0:T(8,128)S(1)} %copy-done.6, ...), custom_call_target="tpu_custom_call" | custom-call | tf_op jit(solution)/shard_map/front/pallas_call | solution.py:311
  61.4 19.4 %place.2.msgs = bf16[64,80,128]{2,1,0:T(8,128)(2,1)S(1)} custom-call(s32[8,512]{1,0:T(8,128)S(1)} %get-tuple-element.39.slots, f32[4096,128]{1,0:T(8,128)S(1)} %get-tuple-element.93.src), custom_call_target="tpu_custom_call" | custom-call | tf_op jit(solution)/shard_map/place/pallas_call | solution.py:369
  80.8 45.4 %bins.2 = (f32[288,128]{1,0:T(8,128)S(1)}, f32[8,128]{1,0:T(8,128)S(1)}) custom-call(bf16[64,80,128]{2,1,0:T(8,128)(2,1)S(1)} %place.2.msgs), custom_call_target="tpu_custom_call" | custom-call | tf_op jit(solution)/shard_map/bins/pallas_call | solution.py:527
  126.2 0.5 slice.6
  127.3 0.7 copy.19
  (1 shorter events, 0.0 us)
Async XLA Ops:
  0.7 1.7 %copy-start = (bf16[80,8,2048]{2,1,0:T(8,128)(2,1)S(1)}, bf16[80,8,2048]{2,1,0:T(8,128)(2,1)}, u32[]{:S(2)}) copy-start(bf16[80,8,2048]{2,1,0:T(8,128)(2,1)} %raw.1) | copy-start | bytes 7864324
  2.5 1.0 copy-start.2
  3.4 1.0 copy-start.3
  4.4 0.8 copy-start.4
  5.3 0.8 copy-start.5
  6.1 0.8 copy-start.6
  6.9 0.8 copy-start.7
  7.8 0.8 copy-start.8
  8.6 0.8 copy-start.9
  9.3 0.7 copy-start.10

commit v3 on v1

v3 whole, which is shorter than its diff:
```python
import functools

import jax
import jax.numpy as jnp
import numpy as np
from jax import lax
from jax.experimental import pallas as pl
from jax.experimental.pallas import tpu as pltpu
from jax.sharding import PartitionSpec as P

F32 = jnp.float32
BF16 = jnp.bfloat16
MESH = pl.DeviceIdType.MESH
VMEM = pltpu.MemorySpace.VMEM
SMEM = pltpu.MemorySpace.SMEM

ROWS8 = 8
W = 2048
FB = 80
TM = 4
QUARTER = W // TM
FRAMES = FB * TM
LAGS = 64
HALF = 36000
BW = 1152
NB = 64
CAP = 128
NDFT = 400
FPAD = 208
MROWS = 80


def dft_tables():
    t = np.arange(FRAMES)
    f = np.arange(NDFT // 2 + 1)
    angle = 2 * np.pi * ((f[:, None] * t[None, :]) % NDFT) / NDFT
    forward = np.zeros((2 * FPAD, FRAMES), np.float64)
    forward[: f.size] = np.cos(angle)
    forward[FPAD : FPAD + f.size] = np.sin(angle)
    k = np.arange(80)
    back = np.zeros((80, FPAD), np.float64)
    fold = np.full(f.size, 2.0)
    fold[0] = fold[-1] = 1.0
    back[:, : f.size] = np.cos(2 * np.pi * ((k[:, None] * f[None, :]) % NDFT) / NDFT) * fold / NDFT

    def split(a):
        hi = a.astype(jnp.bfloat16)
        lo = (a - hi.astype(np.float64)).astype(jnp.bfloat16)
        return hi, lo

    return (*split(forward), *split(back))


def position():
    rows = lax.axis_index("rows")
    tm = lax.axis_index("tm")
    return rows % 4, rows // 8, (tm // 2) * 2 + (rows // 4) % 2, tm % 2


def device(x, y, z, core):
    return (y * 8 + (z % 2) * 4 + x, (z // 2) * 2 + core)


def at_offset(i):
    x, y, z, _ = position()
    i = (i * 37) % NB
    rows, tm = device((x + i % 4) % 4, (y + (i // 4) % 4) % 4, (z + i // 16) % 4, 0)
    return rows, tm // 2


def signal(sem, where):
    pl.semaphore_signal(sem, inc=1, device_id=where, device_id_type=MESH)


def spread_partner(k):
    x, y, z, core = position()
    return (
        lambda: device(x, y, z, 1 - core),
        lambda: device((x + 1) % 4, y, z, core),
        lambda: device((x + 2) % 4, y, z, core),
        lambda: device(x, (y + 1) % 4, z, core),
        lambda: device(x, (y + 2) % 4, z, core),
        lambda: device(x, y, (z + 1) % 4, core),
        lambda: device(x, y, (z + 2) % 4, core),
    )[k]()


SPREAD = 7


def spread_round(k, sems):
    if k > 0:
        pl.semaphore_wait(sems.at[k - 1], 1)
    if k < SPREAD:
        signal(sems.at[k], spread_partner(k))


def greet_near(barrier):
    x, y, z, core = position()
    for where in (
        device(x, y, z, 1 - core),
        device((x + 1) % 4, y, z, core),
        device((x + 3) % 4, y, z, core),
        device((x + 2) % 4, y, z, core),
        device(x, (y + 1) % 4, z, core),
        device(x, (y + 3) % 4, z, core),
        device(x, (y + 2) % 4, z, core),
        device(x, y, (z + 2) % 4, core),
    ):
        signal(barrier, where)
    return 8


def smooth_block(taps, wp, out, i, fb):
    lane = lax.broadcasted_iota(jnp.int32, (16, 128), 1)
    zero = jnp.zeros((16, 128), F32)
    chunks = W // 128
    frames = pl.ds(pl.multiple_of(fb * 16, 16), 16)
    rolled = []

    def finish(c):
        left = rolled[c - 1] if c > 0 else (zero,) * 5
        right = rolled[c + 1] if c + 1 < chunks else (zero,) * 5
        mine = rolled[c]
        total = mine[2]
        total = total + jnp.where(lane >= 2, mine[0], left[0])
        total = total + jnp.where(lane >= 1, mine[1], left[1])
        total = total + jnp.where(lane < 127, mine[3], right[3])
        total = total + jnp.where(lane < 126, mine[4], right[4])
        out[i, frames, c * 128 : (c + 1) * 128] = total.astype(BF16)

    for c in range(chunks):
        rows = [wp[i + a, frames, c * 128 : (c + 1) * 128].astype(F32) for a in range(5)]
        part = []
        for b in range(5):
            acc = rows[0] * taps[0, b]
            for a in range(1, 5):
                acc = acc + rows[a] * taps[a, b]
            part.append(acc)
        rolled.append(
            (
                pltpu.roll(part[0], 2, 1),
                pltpu.roll(part[1], 1, 1),
                part[2],
                pltpu.roll(part[3], 127, 1),
                pltpu.roll(part[4], 126, 1),
            )
        )
        if c >= 1:
            finish(c - 1)
    finish(chunks - 1)


def bucket_of(label):
    half = label >= HALF
    inside = jnp.where(half, label - HALF, label)
    quotient = lax.shift_right_logical(lax.shift_right_logical(inside, 7) * 57, 9)
    bucket = jnp.where(half, quotient + 32, quotient)
    return bucket, inside - quotient * BW


def fill_slots(labels, first, buckets, ranks, parts=None):
    upper = (
        lax.broadcasted_iota(jnp.int32, (QUARTER, QUARTER), 0)
        <= lax.broadcasted_iota(jnp.int32, (QUARTER, QUARTER), 1)
    ).astype(F32).astype(BF16)
    which = lax.broadcasted_iota(jnp.int32, (NB, QUARTER), 0)
    sub = lax.broadcasted_iota(jnp.int32, (8, QUARTER), 0)
    carry = jnp.zeros((NB, 1), F32)
    for i in range(ROWS8):
        bucket, local = bucket_of(labels[i : i + 1, :])
        hot = (which == bucket).astype(F32)
        count = jnp.dot(hot.astype(BF16), upper, preferred_element_type=F32) + carry
        rank = jnp.sum(hot * count, axis=0, keepdims=True) - 1.0 - first
        ranks[i : i + 1, :] = jnp.where((rank >= 0) & (rank < CAP), rank, -1024.0)
        buckets[i : i + 1, :] = bucket.astype(F32)
        if parts is not None:
            top = lax.shift_right_logical(local, 7)
            low = local - top * 128
            parts[i] = jnp.where(sub == 0, top.astype(F32), jnp.where(sub == 1, low.astype(F32), 0.0))
        carry = count[:, QUARTER - 1 : QUARTER]
    most = jnp.max(carry, axis=0, keepdims=True)
    return lax.shift_right_logical(most.astype(jnp.int32) + (CAP - 1), 7).astype(F32)


def route_and_bin(values, buckets, ranks, out, most, msgs, recv, acc, tops, fin, got, sems):
    send_sem, recv_sem, fsend, frecv, own_sem = sems
    rows_me = lax.axis_index("rows")
    tm_me = lax.axis_index("tm")
    core = tm_me % 2
    chip = rows_me * 2 + tm_me // 2

    def route(i):
        rows, zh = at_offset(i)
        return pltpu.make_async_remote_copy(
            src_ref=msgs.at[i],
            dst_ref=recv.at[i],
            send_sem=send_sem.at[i],
            recv_sem=recv_sem.at[i],
            device_id=(rows, zh * 2 + core),
            device_id_type=MESH,
        )

    def chip_at(i):
        rows, zh = at_offset(i)
        return (rows * 2 + zh).astype(F32)

    slot_id = lax.broadcasted_iota(jnp.int32, (2 * CAP, QUARTER), 0).astype(F32)

    def fill(g):
        first, second = chip_at(2 * g), chip_at(2 * g + 1)
        b = buckets[...]
        r = ranks[...]
        key = jnp.where(b == first, r, jnp.where(b == second, r + CAP, -1.0))
        total = jnp.zeros((MROWS, 2 * CAP), F32)
        for i in range(ROWS8):
            hot = jnp.where(slot_id == key[i : i + 1, :], 1.0, 0.0).astype(BF16)
            total = total + lax.dot_general(
                values[i], hot, (((1,), (1,)), ((), ())), preferred_element_type=F32
            )
        return total.astype(BF16)

    both = fill(0)
    recv[0] = both[:, :CAP]
    msgs[1] = both[:, CAP:]
    route(1).start()

    def send(g, carry):
        both = fill(g)
        msgs[2 * g] = both[:, :CAP]
        msgs[2 * g + 1] = both[:, CAP:]
        route(2 * g).start()
        route(2 * g + 1).start()
        return carry

    lax.fori_loop(1, NB // 2, send, 0)

    acc[...] = jnp.zeros_like(acc)
    tops[...] = jnp.zeros_like(tops)
    row_id = lax.broadcasted_iota(jnp.int32, (128, 2 * CAP), 0).astype(F32)

    def add(first, second):
        both = jnp.concatenate([first, second], axis=1)
        extra = both[LAGS : LAGS + 16].astype(F32)
        high, low = extra[0:1], extra[1:2]
        tops[...] = jnp.maximum(tops[...], extra[2:3])
        for h in range(BW // 128):
            key = jnp.where(high == h, low, -1.0)
            hot = jnp.where(row_id == key, 1.0, 0.0).astype(BF16)
            acc[:, h * 128 : (h + 1) * 128] += lax.dot_general(
                both[:LAGS], hot, (((1,), (1,)), ((), ())), preferred_element_type=F32
            )

    route(1).wait_recv()
    add(recv[0], recv[1])

    def pair(g, carry):
        i = 2 * g
        route(i).wait_recv()
        route(i + 1).wait_recv()
        add(recv[i], recv[i + 1])
        return carry

    lax.fori_loop(1, NB // 2, pair, 0)

    for h in range(BW // 128):
        fin[:, h, :] = acc[:, h * 128 : (h + 1) * 128]
    peak = jnp.max(tops[...], axis=1, keepdims=True)
    fin[:, BW // 128, :] = jnp.broadcast_to(peak, (LAGS, 128))

    half = chip // 32
    spot = core * 32 + chip % 32

    def owner(i):
        rows, zh = at_offset(i)
        return pltpu.make_async_remote_copy(
            src_ref=fin.at[rows * 2 + zh],
            dst_ref=got.at[spot],
            send_sem=fsend.at[i],
            recv_sem=frecv.at[spot],
            device_id=(rows, zh * 2 + half),
            device_id_type=MESH,
        )

    def hand(i, carry):
        owner(i).start()
        return carry

    lax.fori_loop(1, NB, hand, 0)

    own = pltpu.make_async_copy(fin.at[chip], got.at[spot], frecv.at[spot])

    @pl.when(half == core)
    def _():
        own.start()

    @pl.when(half != core)
    def _():
        owner(0).start()

    def arrived(n, carry):
        pltpu.make_async_copy(got.at[n], got.at[n], frecv.at[n]).wait()
        return carry

    lax.fori_loop(0, NB, arrived, 0)

    top = jnp.zeros((1, 128), F32)
    for j in range(32):
        out[9 * j : 9 * j + 9, :] = got[j, 0:9, :] + got[32 + j, 0:9, :]
        top = jnp.maximum(top, jnp.maximum(got[j, 9:10, :], got[32 + j, 9:10, :]))
    most[...] = jnp.broadcast_to(top, (8, 128))

    def drain(i, carry):
        route(i).wait_send()
        owner(i).wait_send()
        return carry

    lax.fori_loop(1, NB, drain, 0)

    @pl.when(half != core)
    def _():
        owner(0).wait_send()


def route_scratch():
    dma = pltpu.SemaphoreType.DMA
    return [
        pltpu.VMEM((NB, MROWS, CAP), BF16),
        pltpu.VMEM((NB, MROWS, CAP), BF16),
        pltpu.VMEM((LAGS, BW), F32),
        pltpu.VMEM((1, 2 * CAP), F32),
        pltpu.VMEM((LAGS, BW // 128 + 1, 128), F32),
        pltpu.VMEM((NB, BW // 128 + 1, 128), F32),
        dma((NB,)),
        dma((NB,)),
        dma((NB,)),
        dma((NB,)),
        dma(()),
    ]


SUMS = (
    jax.ShapeDtypeStruct((32 * BW // 128, 128), F32),
    jax.ShapeDtypeStruct((8, 128), F32),
)


def again_kernel(step_ref, values, labels, out, most, buckets, ranks, spread, *scratch):
    barrier = pltpu.get_barrier_semaphore()
    near = greet_near(barrier)
    x, y, z, core = position()
    signal(barrier, device(x, y, (z + 1) % 4, core))
    signal(barrier, device(x, y, (z + 3) % 4, core))
    pl.semaphore_wait(barrier, near + 2)
    for k in range(SPREAD + 1):
        spread_round(k, spread)
    fill_slots(labels, (step_ref[0, 0] * CAP).astype(F32), buckets, ranks)
    route_and_bin(values, buckets, ranks, out, most, *scratch[:6], scratch[6:])


def another_round(step, values, labels):
    return pl.pallas_call(
        again_kernel,
        out_shape=SUMS,
        in_specs=[
            pl.BlockSpec(memory_space=SMEM),
            pl.BlockSpec(memory_space=VMEM),
            pl.BlockSpec(memory_space=VMEM),
        ],
        out_specs=(pl.BlockSpec(memory_space=VMEM),) * 2,
        scratch_shapes=[
            pltpu.VMEM((ROWS8, QUARTER), F32),
            pltpu.VMEM((ROWS8, QUARTER), F32),
            pltpu.SemaphoreType.REGULAR((SPREAD,)),
            *route_scratch(),
        ],
        compiler_params=pltpu.CompilerParams(
            collective_id=1, has_side_effects=True, vmem_limit_bytes=40 << 20
        ),
        name="again",
    )(step, values, labels)


def main_kernel(
    taps, raw_in, dark_in, flat_in, gain_in, labels_in, lag_in, fhi_in, flo_in, bhi_in, blo_in,
    out, most, values_out, labels_out,
    raw, dark, flat, gain, all_labels, lag_row, fhi, flo, bhi, blo, in_sem,
    wp, smoothed, series, labels, parts, values, buckets, ranks,
    hsend, hrecv, msend, mrecv, esend, erecv, lsend, lrecv, spread, keep_sem, *scratch,
):
    rows = lax.axis_index("rows")
    tm = lax.axis_index("tm")
    over = rows + 4 - 8 * ((rows // 4) % 2)
    not_first = (rows + 31) // 32
    not_last = 1 - (rows + 1) // 32
    blocks = FB // 16

    ins = [pltpu.make_async_copy(a, b, in_sem.at[n]) for n, (a, b) in enumerate((
        (dark_in, dark), (flat_in, flat), (gain_in, gain), (labels_in, all_labels),
        (lag_in, lag_row), (fhi_in, fhi), (flo_in, flo), (bhi_in, bhi), (blo_in, blo),
    ))]
    raws = [
        pltpu.make_async_copy(raw_in.at[pl.ds(q * 16, 16)], raw.at[pl.ds(q * 16, 16)], in_sem.at[9 + q])
        for q in range(blocks)
    ]
    for copy in ins[:3]:
        copy.start()
    for copy in raws:
        copy.start()
    for copy in ins[3:]:
        copy.start()

    barrier = pltpu.get_barrier_semaphore()

    @pl.when(rows > 0)
    def _():
        signal(barrier, (rows - 1, tm))

    @pl.when(rows < 31)
    def _():
        signal(barrier, (rows + 1, tm))

    for q in range(TM):
        signal(barrier, (over, q))
    near = greet_near(barrier)

    def to_next(q):
        frames = pl.ds(pl.multiple_of(q * 16, 16), 16)
        return pltpu.make_async_remote_copy(
            src_ref=wp.at[8:10, frames], dst_ref=wp.at[0:2, frames],
            send_sem=hsend.at[0, q], recv_sem=hrecv.at[0, q],
            device_id=(rows + 1, tm), device_id_type=MESH,
        )

    def to_previous(q):
        frames = pl.ds(pl.multiple_of(q * 16, 16), 16)
        return pltpu.make_async_remote_copy(
            src_ref=wp.at[2:4, frames], dst_ref=wp.at[10:12, frames],
            send_sem=hsend.at[1, q], recv_sem=hrecv.at[1, q],
            device_id=(rows - 1, tm), device_id_type=MESH,
        )

    label_copy = pltpu.make_async_remote_copy(
        src_ref=all_labels.at[:, pl.ds(pl.multiple_of(tm * QUARTER, QUARTER), QUARTER)],
        dst_ref=labels, send_sem=lsend, recv_sem=lrecv,
        device_id=(over, tm), device_id_type=MESH,
    )

    @pl.when(rows == 0)
    def _():
        wp[0:2] = jnp.zeros((2, FB, W), BF16)

    @pl.when(rows == 31)
    def _():
        wp[10:12] = jnp.zeros((2, FB, W), BF16)

    for copy in ins[:3]:
        copy.wait()
    cols = 256
    for q in range(blocks):
        raws[q].wait()

        def weigh(c, carry):
            at = pl.ds(pl.multiple_of(c * cols, cols), cols)
            v = raw[q * 16 : (q + 1) * 16, :, at].astype(F32)
            v = (v - dark[:, at][None]) * flat[:, at][None] * gain[:, at][None]
            wp[2:10, q * 16 : (q + 1) * 16, at] = jnp.swapaxes(v, 0, 1).astype(BF16)
            return carry

        lax.fori_loop(0, W // cols, weigh, 0)

        if q == 0:
            pl.semaphore_wait(barrier, near + TM + not_first + not_last)

        @pl.when(rows < 31)
        def _():
            to_next(q).start()

        @pl.when(rows > 0)
        def _():
            to_previous(q).start()

    ins[3].wait()
    label_copy.start()

    def mine(t):
        return pl.ds(pl.multiple_of(t * FB, FB), FB)

    def across(i, q):
        return pltpu.make_async_remote_copy(
            src_ref=smoothed.at[i, :, q * QUARTER : (q + 1) * QUARTER],
            dst_ref=series.at[i, mine(tm), :],
            send_sem=msend.at[i, q], recv_sem=mrecv.at[i, tm],
            device_id=(over, q), device_id_type=MESH,
        )

    def across_edge(e, fb, q):
        return pltpu.make_async_remote_copy(
            src_ref=smoothed.at[
                pl.ds(6 * e, 2), pl.ds(pl.multiple_of(fb * 16, 16), 16), q * QUARTER : (q + 1) * QUARTER
            ],
            dst_ref=series.at[pl.ds(6 * e, 2), pl.ds(pl.multiple_of(tm * FB + fb * 16, 16), 16), :],
            send_sem=esend.at[e, fb, q], recv_sem=erecv.at[e, fb, tm],
            device_id=(over, q), device_id_type=MESH,
        )

    def middle(i, carry):
        for k in range(4):

            @pl.when(i == k + 2)
            def _():
                spread_round(k, spread)

        def one(fb, c):
            smooth_block(taps, wp, smoothed, i, fb)
            return c

        lax.fori_loop(0, blocks, one, 0)
        for q in range(TM):
            across(i, q).start()
        return carry

    lax.fori_loop(2, 6, middle, 0)

    def edges(n, carry):
        fb = n // 2
        e = n % 2
        for k in range(4, SPREAD + 1):

            @pl.when(n == 2 * (k - 4))
            def _():
                spread_round(k, spread)

        @pl.when((e == 0) & (rows > 0))
        def _():
            to_next(fb).wait_recv()

        @pl.when((e == 1) & (rows < 31))
        def _():
            to_previous(fb).wait_recv()

        def one(j, c):
            smooth_block(taps, wp, smoothed, 6 * e + j, fb)
            return c

        lax.fori_loop(0, 2, one, 0)
        for q in range(TM):
            across_edge(e, fb, q).start()
        return carry

    lax.fori_loop(0, 2 * blocks, edges, 0)

    label_copy.wait_recv()
    keep_labels = pltpu.make_async_copy(labels, labels_out, keep_sem.at[0])
    keep_labels.start()
    rounds = fill_slots(labels, 0.0, buckets, ranks, parts)

    for copy in ins[4:]:
        copy.wait()
    turned = (
        lax.broadcasted_iota(jnp.int32, (128, LAGS), 0) == lag_row[...]
    ).astype(F32).T
    pick = turned[:, :80].astype(BF16)
    lag = jnp.sum(
        turned * lax.broadcasted_iota(jnp.int32, (LAGS, 128), 1).astype(F32), axis=1, keepdims=True
    )
    chi = jnp.dot(pick, bhi[...], preferred_element_type=F32).astype(BF16)
    clo = jnp.dot(pick, blo[...], preferred_element_type=F32).astype(BF16)
    scale = 1.0 / (FRAMES - lag)
    sub = lax.broadcasted_iota(jnp.int32, (8, QUARTER), 0)

    def lags(i, carry):
        s = series[i]
        x = jnp.dot(fhi[...], s, preferred_element_type=F32)
        x = x + jnp.dot(flo[...], s, preferred_element_type=F32)
        power = x[:FPAD] * x[:FPAD] + x[FPAD:] * x[FPAD:]
        phi = power.astype(BF16)
        plo = (power - phi.astype(F32)).astype(BF16)
        r = jnp.dot(chi, phi, preferred_element_type=F32)
        r = r + jnp.dot(chi, plo, preferred_element_type=F32)
        r = r + jnp.dot(clo, phi, preferred_element_type=F32)
        r = r * scale
        extra = jnp.where(sub == 2, rounds, parts[i])
        full = jnp.concatenate([r, extra, jnp.zeros((MROWS - LAGS - 8, QUARTER), F32)], axis=0)
        values[i] = full.astype(BF16)
        return carry

    def middle_lags(i, carry):
        for t in range(TM):
            part = series.at[i, pl.ds(t * FB, FB)]
            pltpu.make_async_copy(part, part, mrecv.at[i, t]).wait()
        return lags(i, carry)

    lax.fori_loop(2, 6, middle_lags, 0)

    def edge_lags(e, carry):
        for t in range(TM):
            for fb in range(blocks):
                part = series.at[pl.ds(6 * e, 2), pl.ds(t * FB + fb * 16, 16)]
                pltpu.make_async_copy(part, part, erecv.at[e, fb, t]).wait()
        lags(6 * e, carry)
        return lags(6 * e + 1, carry)

    lax.fori_loop(0, 2, edge_lags, 0)
    keep_values = pltpu.make_async_copy(values, values_out, keep_sem.at[1])
    keep_values.start()

    route_and_bin(values, buckets, ranks, out, most, *scratch[:6], scratch[6:])

    def drain(i, carry):
        for q in range(TM):
            across(i, q).wait_send()
        return carry

    lax.fori_loop(2, 6, drain, 0)

    def drain_edges(n, carry):
        for q in range(TM):
            across_edge(n % 2, n // 2, q).wait_send()
        return carry

    lax.fori_loop(0, 2 * blocks, drain_edges, 0)
    label_copy.wait_send()
    for q in range(blocks):

        @pl.when(rows < 31)
        def _():
            to_next(q).wait_send()

        @pl.when(rows > 0)
        def _():
            to_previous(q).wait_send()

    keep_labels.wait()
    keep_values.wait()


def first_round(taps, raw, dark, flat, gain, labels, lag_row, tables):
    dma = pltpu.SemaphoreType.DMA
    hbm = pl.BlockSpec(memory_space=pltpu.MemorySpace.HBM)
    vmem = pl.BlockSpec(memory_space=VMEM)
    blocks = FB // 16
    plane = (ROWS8, W)
    return pl.pallas_call(
        main_kernel,
        out_shape=(
            *SUMS,
            jax.ShapeDtypeStruct((ROWS8, MROWS, QUARTER), BF16),
            jax.ShapeDtypeStruct((ROWS8, QUARTER), jnp.int32),
        ),
        in_specs=[pl.BlockSpec(memory_space=SMEM)] + [hbm] * 10,
        out_specs=(vmem, vmem, hbm, hbm),
        scratch_shapes=[
            pltpu.VMEM((FB, ROWS8, W), BF16),
            pltpu.VMEM(plane, F32),
            pltpu.VMEM(plane, F32),
            pltpu.VMEM(plane, F32),
            pltpu.VMEM(plane, jnp.int32),
            pltpu.VMEM((1, LAGS), jnp.int32),
            pltpu.VMEM((2 * FPAD, FRAMES), BF16),
            pltpu.VMEM((2 * FPAD, FRAMES), BF16),
            pltpu.VMEM((80, FPAD), BF16),
            pltpu.VMEM((80, FPAD), BF16),
            dma((9 + blocks,)),
            pltpu.VMEM((ROWS8 + 4, FB, W), BF16),
            pltpu.VMEM((ROWS8, FB, W), BF16),
            pltpu.VMEM((ROWS8, FRAMES, QUARTER), BF16),
            pltpu.VMEM((ROWS8, QUARTER), jnp.int32),
            pltpu.VMEM((ROWS8, 8, QUARTER), F32),
            pltpu.VMEM((ROWS8, MROWS, QUARTER), BF16),
            pltpu.VMEM((ROWS8, QUARTER), F32),
            pltpu.VMEM((ROWS8, QUARTER), F32),
            dma((2, blocks)),
            dma((2, blocks)),
            dma((ROWS8, TM)),
            dma((ROWS8, TM)),
            dma((2, blocks, TM)),
            dma((2, blocks, TM)),
            dma(()),
            dma(()),
            pltpu.SemaphoreType.REGULAR((SPREAD,)),
            dma((2,)),
            *route_scratch(),
        ],
        compiler_params=pltpu.CompilerParams(
            collective_id=0, has_side_effects=True, vmem_limit_bytes=56 << 20
        ),
        name="first",
    )(taps, raw, dark, flat, gain, labels, lag_row, *tables)


def per_device(
    raw_frames, dark_frame, flat_field, pixel_gain, smoothing_kernel, bin_labels, lag_list
):
    tables = [jnp.asarray(a) for a in dft_tables()]
    sums, most, values, labels = first_round(
        smoothing_kernel, raw_frames, dark_frame, flat_field, pixel_gain, bin_labels,
        lag_list.reshape(1, LAGS), tables,
    )
    needed = most[0, 0].astype(jnp.int32)

    def more(state):
        return state[0] < needed

    def again(state):
        step, total = state
        extra, _ = another_round(step.reshape(1, 1), values, labels)
        return step + 1, total + extra

    _, sums = lax.while_loop(more, again, (jnp.int32(1), sums))
    return sums.reshape(-1)[:HALF]


def solution(mesh):
    return jax.shard_map(
        per_device,
        mesh=mesh,
        in_specs=(
            P("tm", "rows", None),
            P("rows", None),
            P("rows", None),
            P("rows", None),
            P(),
            P("rows", None),
            P(),
        ),
        out_specs=P(("rows", "tm")),
        check_vma=False,
    )
```

time: 182 us -> 112 us (0.62)
  waiting for transfers between devices: 63.2 us -> 0 us
  Pallas kernels: 88.6 us -> 109 us
  starting transfers between devices: 12.4 us -> 0 us
  local copies, waits for them, and re-layouts: 12 us -> 1.87 us
  other arithmetic: 3.53 us -> 0 us
    all_to_all x1 -> x0, waiting for transfers between devices: 47.3 us -> none  [per_device(): lax.all_to_all(smoothed, 'tm', split_axis=2, concat_axis=1, tiled=True)]
    pallas_call x4 -> x1, Pallas kernels: 88.6 us -> 109 us  [first_round(): pl.pallas_call(main_kernel, out_shape=(*SUMS, jax.ShapeDtypeStruct((ROWS8...]
    ppermute x2 -> x0, waiting for transfers between devices: 15.9 us -> none  [the longest x1 12.1 us: per_device(): before = lax.ppermute(weighted[ROWS8 - 2:], 'rows', up)]
    all_to_all x1 -> x0, starting transfers between devices: 7.08 us -> none  [per_device(): lax.all_to_all(smoothed, 'tm', split_axis=2, concat_axis=1, tiled=True)]
    all_to_all x1 -> x0, local copies, waits for them, and re-layouts: 5.82 us -> none  [per_device(): lax.all_to_all(smoothed, 'tm', split_axis=2, concat_axis=1, tiled=True)]
    ppermute x2 -> x0, starting transfers between devices: 5.27 us -> none  [the longest x1 3.97 us: per_device(): before = lax.ppermute(weighted[ROWS8 - 2:], 'rows', up)]
    pallas_call x1 -> x0, local copies, waits for them, and re-layouts: 4.75 us -> none  [smooth(): pl.pallas_call(smooth_kernel, out_shape=jax.ShapeDtypeStruct((ROWS8, FB,...]
    transpose x1 -> x0, other arithmetic: 3.53 us -> none  [per_device(): weighted = jnp.transpose(weighted, (1, 0, 2))]
  transfers between devices with their start and end apart: 3 -> 0, of which waited for: 3 -> 0; matrix products, arithmetic and copies ran while one was open for 0% -> 0% of each run, Pallas kernels for 1% -> 0%
where the time goes in v3:
time: 112 us
  Pallas kernels  109 us (97%)
  local copies, waits for them, and re-layouts  1.87 us (2%)
    pallas_call x1, Pallas kernels, first_round(): pl.pallas_call(main_kernel, out_shape=(*SUMS, jax.ShapeDtypeStruct((ROWS8...  109 us

profile of v3, /device:TPU:1, one launch (start us, length us, event | category | flops | bytes accessed | tf_op | source)
XLA Modules:
  0.0 111.9 jit_solution(2529733676945764164)
XLA Ops:
  0.0 109.3 %first.1 = (f32[288,128]{1,0:T(8,128)S(1)}, f32[8,128]{1,0:T(8,128)}, bf16[8,80,512]{2,1,0:T(8,128)(2,1)S(1)}, s32[8,512]{1,0:T(8,128)S(1)}) custom-call(f32[5,5]{1,0:T(8,128)} %taps.1, bf16[80,8,2048]{2,1,0:T(8,128)(2,1)} %raw_in.1, f32[8,2048]{1,0:T(8,128)} %dark_in.1, f32[8,2048]{1,0:T(8,128)} %flat_in.1, f32[8,2048]{1,0:T(8,128)} %gain_in.1, ...), custom_call_target="tpu_custom_call" | custom-call | tf_op jit(solution)/shard_map/first/pallas_call | solution.py:644
  109.3 1.2 %slice.6 = f32[1,1]{1,0:T(1,128)} slice(f32[8,128]{1,0:T(8,128)} %get-tuple-element.39), slice={[0:1], [0:1]} | slice | bytes 8 | tf_op jit(solution)/shard_map/slice | solution.py:700
  111.2 0.7 copy.19
  (1 shorter events, 0.0 us)

commit v4 on v3

--- a/solution.py
+++ b/solution.py
@@ -27,7 +27,7 @@
 CAP = 128
 NDFT = 400
 FPAD = 208
-MROWS = 80
+MROWS = 72
 
 
 def dft_tables():
@@ -183,7 +183,38 @@
     return lax.shift_right_logical(most.astype(jnp.int32) + (CAP - 1), 7).astype(F32)
 
 
-def route_and_bin(values, buckets, ranks, out, most, msgs, recv, acc, tops, fin, got, sems):
+def chip_at(i):
+    rows, zh = at_offset(i)
+    return (rows * 2 + zh).astype(F32)
+
+
+def in_slots(g, rows, values, buckets, ranks):
+    slot_id = lax.broadcasted_iota(jnp.int32, (2 * CAP, QUARTER), 0).astype(F32)
+    b = buckets[...]
+    r = ranks[...]
+    key = jnp.where(b == chip_at(2 * g), r, jnp.where(b == chip_at(2 * g + 1), r + CAP, -1.0))
+    total = jnp.zeros((MROWS, 2 * CAP), F32)
+    for i in rows:
+        hot = jnp.where(slot_id == key[i : i + 1, :], 1.0, 0.0).astype(BF16)
+        total = total + lax.dot_general(
+            values[i], hot, (((1,), (1,)), ((), ())), preferred_element_type=F32
+        )
+    return total
+
+
+MIDDLE = (2, 3, 4, 5)
+EDGES = (0, 1, 6, 7)
+
+
+def fill_middle(values, buckets, ranks, part):
+    def one(g, carry):
+        part[g] = in_slots(g, MIDDLE, values, buckets, ranks)
+        return carry
+
+    lax.fori_loop(0, NB // 2, one, 0)
+
+
+def route_and_bin(values, buckets, ranks, out, most, part, msgs, recv, acc, tops, fin, got, sems):
     send_sem, recv_sem, fsend, frecv, own_sem = sems
     rows_me = lax.axis_index("rows")
     tm_me = lax.axis_index("tm")
@@ -201,24 +232,8 @@
             device_id_type=MESH,
         )
 
-    def chip_at(i):
-        rows, zh = at_offset(i)
-        return (rows * 2 + zh).astype(F32)
-
-    slot_id = lax.broadcasted_iota(jnp.int32, (2 * CAP, QUARTER), 0).astype(F32)
-
     def fill(g):
-        first, second = chip_at(2 * g), chip_at(2 * g + 1)
-        b = buckets[...]
-        r = ranks[...]
-        key = jnp.where(b == first, r, jnp.where(b == second, r + CAP, -1.0))
-        total = jnp.zeros((MROWS, 2 * CAP), F32)
-        for i in range(ROWS8):
-            hot = jnp.where(slot_id == key[i : i + 1, :], 1.0, 0.0).astype(BF16)
-            total = total + lax.dot_general(
-                values[i], hot, (((1,), (1,)), ((), ())), preferred_element_type=F32
-            )
-        return total.astype(BF16)
+        return (part[g] + in_slots(g, EDGES, values, buckets, ranks)).astype(BF16)
 
     both = fill(0)
     recv[0] = both[:, :CAP]
@@ -241,7 +256,7 @@
 
     def add(first, second):
         both = jnp.concatenate([first, second], axis=1)
-        extra = both[LAGS : LAGS + 16].astype(F32)
+        extra = both[LAGS:MROWS].astype(F32)
         high, low = extra[0:1], extra[1:2]
         tops[...] = jnp.maximum(tops[...], extra[2:3])
         for h in range(BW // 128):
@@ -325,6 +340,7 @@
 def route_scratch():
     dma = pltpu.SemaphoreType.DMA
     return [
+        pltpu.VMEM((NB // 2, MROWS, 2 * CAP), F32),
         pltpu.VMEM((NB, MROWS, CAP), BF16),
         pltpu.VMEM((NB, MROWS, CAP), BF16),
         pltpu.VMEM((LAGS, BW), F32),
@@ -355,7 +371,8 @@
     for k in range(SPREAD + 1):
         spread_round(k, spread)
     fill_slots(labels, (step_ref[0, 0] * CAP).astype(F32), buckets, ranks)
-    route_and_bin(values, buckets, ranks, out, most, *scratch[:6], scratch[6:])
+    fill_middle(values, buckets, ranks, scratch[0])
+    route_and_bin(values, buckets, ranks, out, most, *scratch[:7], scratch[7:])
 
 
 def another_round(step, values, labels):
@@ -581,8 +598,7 @@
         r = r + jnp.dot(clo, phi, preferred_element_type=F32)
         r = r * scale
         extra = jnp.where(sub == 2, rounds, parts[i])
-        full = jnp.concatenate([r, extra, jnp.zeros((MROWS - LAGS - 8, QUARTER), F32)], axis=0)
-        values[i] = full.astype(BF16)
+        values[i] = jnp.concatenate([r, extra], axis=0).astype(BF16)
         return carry
 
     def middle_lags(i, carry):
@@ -592,6 +608,7 @@
         return lags(i, carry)
 
     lax.fori_loop(2, 6, middle_lags, 0)
+    fill_middle(values, buckets, ranks, scratch[0])
 
     def edge_lags(e, carry):
         for t in range(TM):
@@ -605,7 +622,7 @@
     keep_values = pltpu.make_async_copy(values, values_out, keep_sem.at[1])
     keep_values.start()
 
-    route_and_bin(values, buckets, ranks, out, most, *scratch[:6], scratch[6:])
+    route_and_bin(values, buckets, ranks, out, most, *scratch[:7], scratch[7:])
 
     def drain(i, carry):
         for q in range(TM):

time: 112 us -> 104 us (0.929)
  Pallas kernels: 109 us -> 102 us
    pallas_call x1, Pallas kernels: 109 us -> 102 us  [first_round(): pl.pallas_call(main_kernel, out_shape=(*SUMS, jax.ShapeDtypeStruct((ROWS8...]
where the time goes in v4:
time: 104 us
  Pallas kernels  102 us (98%)
  local copies, waits for them, and re-layouts  1.87 us (2%)
    pallas_call x1, Pallas kernels, first_round(): pl.pallas_call(main_kernel, out_shape=(*SUMS, jax.ShapeDtypeStruct((ROWS8...  102 us

profile of v4, /device:TPU:1, one launch (start us, length us, event | category | flops | bytes accessed | tf_op | source)
XLA Modules:
  0.0 104.1 jit_solution(1811176521998619188)
XLA Ops:
  0.0 101.5 %first.1 = (f32[288,128]{1,0:T(8,128)S(1)}, f32[8,128]{1,0:T(8,128)}, bf16[8,72,512]{2,1,0:T(8,128)(2,1)S(1)}, s32[8,512]{1,0:T(8,128)S(1)}) custom-call(f32[5,5]{1,0:T(8,128)} %taps.1, bf16[80,8,2048]{2,1,0:T(8,128)(2,1)} %raw_in.1, f32[8,2048]{1,0:T(8,128)} %dark_in.1, f32[8,2048]{1,0:T(8,128)} %flat_in.1, f32[8,2048]{1,0:T(8,128)} %gain_in.1, ...), custom_call_target="tpu_custom_call" | custom-call | tf_op jit(solution)/shard_map/first/pallas_call | solution.py:661
  101.5 1.2 %slice.6 = f32[1,1]{1,0:T(1,128)} slice(f32[8,128]{1,0:T(8,128)} %get-tuple-element.39), slice={[0:1], [0:1]} | slice | bytes 8 | tf_op jit(solution)/shard_map/slice | solution.py:717
  103.4 0.7 copy.19
  (1 shorter events, 0.0 us)

commit v5 on v4

--- a/solution.py
+++ b/solution.py
@@ -24,6 +24,7 @@
 HALF = 36000
 BW = 1152
 NB = 64
+UNROLL = 8
 CAP = 128
 NDFT = 400
 FPAD = 208
@@ -190,12 +191,13 @@
 
 def in_slots(g, rows, values, buckets, ranks):
     slot_id = lax.broadcasted_iota(jnp.int32, (2 * CAP, QUARTER), 0).astype(F32)
-    b = buckets[...]
-    r = ranks[...]
-    key = jnp.where(b == chip_at(2 * g), r, jnp.where(b == chip_at(2 * g + 1), r + CAP, -1.0))
+    first, second = chip_at(2 * g), chip_at(2 * g + 1)
     total = jnp.zeros((MROWS, 2 * CAP), F32)
     for i in rows:
-        hot = jnp.where(slot_id == key[i : i + 1, :], 1.0, 0.0).astype(BF16)
+        b = buckets[pl.ds(i, 1), :]
+        r = ranks[pl.ds(i, 1), :]
+        key = jnp.where(b == first, r, jnp.where(b == second, r + CAP, -1.0))
+        hot = jnp.where(slot_id == key, 1.0, 0.0).astype(BF16)
         total = total + lax.dot_general(
             values[i], hot, (((1,), (1,)), ((), ())), preferred_element_type=F32
         )
@@ -203,18 +205,18 @@
 
 
 MIDDLE = (2, 3, 4, 5)
-EDGES = (0, 1, 6, 7)
-
-
-def fill_middle(values, buckets, ranks, part):
+
+
+def fill_part(start, stop, rows, values, buckets, ranks, part, more):
     def one(g, carry):
-        part[g] = in_slots(g, MIDDLE, values, buckets, ranks)
-        return carry
-
-    lax.fori_loop(0, NB // 2, one, 0)
-
-
-def route_and_bin(values, buckets, ranks, out, most, part, msgs, recv, acc, tops, fin, got, sems):
+        total = in_slots(g, rows, values, buckets, ranks)
+        part[g] = part[g] + total if more else total
+        return carry
+
+    lax.fori_loop(start, stop, one, 0, unroll=UNROLL)
+
+
+def route_and_bin(last, values, buckets, ranks, out, most, part, msgs, recv, acc, tops, fin, got, sems):
     send_sem, recv_sem, fsend, frecv, own_sem = sems
     rows_me = lax.axis_index("rows")
     tm_me = lax.axis_index("tm")
@@ -233,22 +235,27 @@
         )
 
     def fill(g):
-        return (part[g] + in_slots(g, EDGES, values, buckets, ranks)).astype(BF16)
-
-    both = fill(0)
-    recv[0] = both[:, :CAP]
-    msgs[1] = both[:, CAP:]
-    route(1).start()
+        return (part[g] + in_slots(g, last, values, buckets, ranks)).astype(BF16)
 
     def send(g, carry):
-        both = fill(g)
-        msgs[2 * g] = both[:, :CAP]
-        msgs[2 * g + 1] = both[:, CAP:]
-        route(2 * g).start()
-        route(2 * g + 1).start()
-        return carry
-
-    lax.fori_loop(1, NB // 2, send, 0)
+        made = [fill(4 * g + u) for u in range(4)]
+        for u in range(4):
+            i = 2 * (4 * g + u)
+            msgs[i] = made[u][:, :CAP]
+            msgs[i + 1] = made[u][:, CAP:]
+            if u == 0:
+
+                @pl.when(g > 0)
+                def _():
+                    route(i).start()
+
+            else:
+                route(i).start()
+            route(i + 1).start()
+        return carry
+
+    lax.fori_loop(0, NB // 8, send, 0)
+    recv[0] = msgs[0]
 
     acc[...] = jnp.zeros_like(acc)
     tops[...] = jnp.zeros_like(tops)
@@ -371,8 +378,8 @@
     for k in range(SPREAD + 1):
         spread_round(k, spread)
     fill_slots(labels, (step_ref[0, 0] * CAP).astype(F32), buckets, ranks)
-    fill_middle(values, buckets, ranks, scratch[0])
-    route_and_bin(values, buckets, ranks, out, most, *scratch[:7], scratch[7:])
+    fill_part(0, NB // 2, (0, 1) + MIDDLE, values, buckets, ranks, scratch[0], False)
+    route_and_bin((6, 7), values, buckets, ranks, out, most, *scratch[:7], scratch[7:])
 
 
 def another_round(step, values, labels):
@@ -403,6 +410,7 @@
     out, most, values_out, labels_out,
     raw, dark, flat, gain, all_labels, lag_row, fhi, flo, bhi, blo, in_sem,
     wp, smoothed, series, labels, parts, values, buckets, ranks,
+    rounds, chi, clo, scale,
     hsend, hrecv, msend, mrecv, esend, erecv, lsend, lrecv, spread, keep_sem, *scratch,
 ):
     rows = lax.axis_index("rows")
@@ -539,90 +547,107 @@
 
     lax.fori_loop(2, 6, middle, 0)
 
-    def edges(n, carry):
-        fb = n // 2
-        e = n % 2
-        for k in range(4, SPREAD + 1):
-
-            @pl.when(n == 2 * (k - 4))
-            def _():
-                spread_round(k, spread)
-
-        @pl.when((e == 0) & (rows > 0))
-        def _():
-            to_next(fb).wait_recv()
-
-        @pl.when((e == 1) & (rows < 31))
-        def _():
-            to_previous(fb).wait_recv()
-
-        def one(j, c):
-            smooth_block(taps, wp, smoothed, 6 * e + j, fb)
-            return c
-
-        lax.fori_loop(0, 2, one, 0)
-        for q in range(TM):
-            across_edge(e, fb, q).start()
-        return carry
-
-    lax.fori_loop(0, 2 * blocks, edges, 0)
-
-    label_copy.wait_recv()
+    sub = lax.broadcasted_iota(jnp.int32, (8, QUARTER), 0)
     keep_labels = pltpu.make_async_copy(labels, labels_out, keep_sem.at[0])
-    keep_labels.start()
-    rounds = fill_slots(labels, 0.0, buckets, ranks, parts)
-
-    for copy in ins[4:]:
-        copy.wait()
-    turned = (
-        lax.broadcasted_iota(jnp.int32, (128, LAGS), 0) == lag_row[...]
-    ).astype(F32).T
-    pick = turned[:, :80].astype(BF16)
-    lag = jnp.sum(
-        turned * lax.broadcasted_iota(jnp.int32, (LAGS, 128), 1).astype(F32), axis=1, keepdims=True
-    )
-    chi = jnp.dot(pick, bhi[...], preferred_element_type=F32).astype(BF16)
-    clo = jnp.dot(pick, blo[...], preferred_element_type=F32).astype(BF16)
-    scale = 1.0 / (FRAMES - lag)
-    sub = lax.broadcasted_iota(jnp.int32, (8, QUARTER), 0)
-
-    def lags(i, carry):
+
+    def prepare():
+        label_copy.wait_recv()
+        keep_labels.start()
+        needed = fill_slots(labels, 0.0, buckets, ranks, parts)
+        rounds[...] = jnp.broadcast_to(needed, (8, 128))
+        for copy in ins[4:]:
+            copy.wait()
+        turned = (lax.broadcasted_iota(jnp.int32, (128, LAGS), 0) == lag_row[...]).astype(F32).T
+        pick = turned[:, :80].astype(BF16)
+        lag = jnp.sum(
+            turned * lax.broadcasted_iota(jnp.int32, (LAGS, 128), 1).astype(F32),
+            axis=1, keepdims=True,
+        )
+        chi[...] = jnp.dot(pick, bhi[...], preferred_element_type=F32).astype(BF16)
+        clo[...] = jnp.dot(pick, blo[...], preferred_element_type=F32).astype(BF16)
+        scale[...] = jnp.broadcast_to(1.0 / (FRAMES - lag), (LAGS, 128))
+
+    def lags(i):
         s = series[i]
         x = jnp.dot(fhi[...], s, preferred_element_type=F32)
         x = x + jnp.dot(flo[...], s, preferred_element_type=F32)
         power = x[:FPAD] * x[:FPAD] + x[FPAD:] * x[FPAD:]
         phi = power.astype(BF16)
         plo = (power - phi.astype(F32)).astype(BF16)
-        r = jnp.dot(chi, phi, preferred_element_type=F32)
-        r = r + jnp.dot(chi, plo, preferred_element_type=F32)
-        r = r + jnp.dot(clo, phi, preferred_element_type=F32)
-        r = r * scale
-        extra = jnp.where(sub == 2, rounds, parts[i])
+        r = jnp.dot(chi[...], phi, preferred_element_type=F32)
+        r = r + jnp.dot(chi[...], plo, preferred_element_type=F32)
+        r = r + jnp.dot(clo[...], phi, preferred_element_type=F32)
+        r = r * scale[:, :1]
+        extra = jnp.where(sub == 2, rounds[:1, :1], parts[i])
         values[i] = jnp.concatenate([r, extra], axis=0).astype(BF16)
-        return carry
-
-    def middle_lags(i, carry):
+
+    def middle_lags(i):
         for t in range(TM):
             part = series.at[i, pl.ds(t * FB, FB)]
             pltpu.make_async_copy(part, part, mrecv.at[i, t]).wait()
-        return lags(i, carry)
-
-    lax.fori_loop(2, 6, middle_lags, 0)
-    fill_middle(values, buckets, ranks, scratch[0])
-
-    def edge_lags(e, carry):
+        lags(i)
+
+    def edge_lags(e):
         for t in range(TM):
             for fb in range(blocks):
                 part = series.at[pl.ds(6 * e, 2), pl.ds(t * FB + fb * 16, 16)]
                 pltpu.make_async_copy(part, part, erecv.at[e, fb, t]).wait()
-        lags(6 * e, carry)
-        return lags(6 * e + 1, carry)
-
-    lax.fori_loop(0, 2, edge_lags, 0)
+
+        def one(j, c):
+            lags(6 * e + j)
+            return c
+
+        lax.fori_loop(0, 2, one, 0)
+
+    flip = 1 - (rows % 4 + 3) // 4
+
+    def edges(n, carry):
+        fb = n % blocks
+        e = (n // blocks + flip) % 2
+        for k in range(4, SPREAD + 1):
+
+            @pl.when(n == k - 4)
+            def _():
+                spread_round(k, spread)
+
+        @pl.when((e == 0) & (rows > 0))
+        def _():
+            to_next(fb).wait_recv()
+
+        @pl.when((e == 1) & (rows < 31))
+        def _():
+            to_previous(fb).wait_recv()
+
+        def one(j, c):
+            smooth_block(taps, wp, smoothed, 6 * e + j, fb)
+            return c
+
+        lax.fori_loop(0, 2, one, 0)
+        for q in range(TM):
+            across_edge(e, fb, q).start()
+
+        @pl.when(n == 0)
+        def _():
+            prepare()
+
+        return carry
+
+    lax.fori_loop(0, 2 * blocks, edges, 0)
+
+    def middle(i, carry):
+        middle_lags(i)
+        return carry
+
+    lax.fori_loop(2, 6, middle, 0)
+    fill_part(0, NB // 2, MIDDLE, values, buckets, ranks, scratch[0], False)
+    edge_lags(flip)
+    fill_part(0, NB // 2, (6 * flip, 6 * flip + 1), values, buckets, ranks, scratch[0], True)
+    last = 1 - flip
+    edge_lags(last)
     keep_values = pltpu.make_async_copy(values, values_out, keep_sem.at[1])
     keep_values.start()
 
-    route_and_bin(values, buckets, ranks, out, most, *scratch[:7], scratch[7:])
+    route_and_bin((6 * last, 6 * last + 1), values, buckets, ranks, out, most, *scratch[:7], scratch[7:])
 
     def drain(i, carry):
         for q in range(TM):
@@ -687,6 +712,10 @@
             pltpu.VMEM((ROWS8, MROWS, QUARTER), BF16),
             pltpu.VMEM((ROWS8, QUARTER), F32),
             pltpu.VMEM((ROWS8, QUARTER), F32),
+            pltpu.VMEM((8, 128), F32),
+            pltpu.VMEM((LAGS, FPAD), BF16),
+            pltpu.VMEM((LAGS, FPAD), BF16),
+            pltpu.VMEM((LAGS, 128), F32),
             dma((2, blocks)),
             dma((2, blocks)),
             dma((ROWS8, TM)),

time: 104 us -> 97.1 us (0.934)
  Pallas kernels: 102 us -> 94.3 us
    pallas_call x1, Pallas kernels: 102 us -> 94.3 us  [first_round(): pl.pallas_call(main_kernel, out_shape=(*SUMS, jax.ShapeDtypeStruct((ROWS8...]
where the time goes in v5:
time: 97.1 us; the launch traced here: 97 us
  Pallas kernels  94.3 us (97%)
  local copies, waits for them, and re-layouts  1.87 us (2%)
    pallas_call x1, Pallas kernels, first_round(): pl.pallas_call(main_kernel, out_shape=(*SUMS, jax.ShapeDtypeStruct((ROWS8...  94.3 us

profile of v5, /device:TPU:1, one launch (start us, length us, event | category | flops | bytes accessed | tf_op | source)
XLA Modules:
  0.0 97.0 jit_solution(10452125781309351309)
XLA Ops:
  0.0 94.3 %first.1 = (f32[288,128]{1,0:T(8,128)S(1)}, f32[8,128]{1,0:T(8,128)}, bf16[8,72,512]{2,1,0:T(8,128)(2,1)S(1)}, s32[8,512]{1,0:T(8,128)S(1)}) custom-call(f32[5,5]{1,0:T(8,128)} %taps.1, bf16[80,8,2048]{2,1,0:T(8,128)(2,1)} %raw_in.1, f32[8,2048]{1,0:T(8,128)} %dark_in.1, f32[8,2048]{1,0:T(8,128)} %flat_in.1, f32[8,2048]{1,0:T(8,128)} %gain_in.1, ...), custom_call_target="tpu_custom_call" | custom-call | tf_op jit(solution)/shard_map/first/pallas_call | solution.py:686
  94.3 1.2 %slice.6 = f32[1,1]{1,0:T(1,128)} slice(f32[8,128]{1,0:T(8,128)} %get-tuple-element.39), slice={[0:1], [0:1]} | slice | bytes 8 | tf_op jit(solution)/shard_map/slice | solution.py:746
  96.1 0.2 while.10
  96.3 0.7 copy.19

commit v6 on v5

--- a/solution.py
+++ b/solution.py
@@ -266,24 +266,35 @@
         extra = both[LAGS:MROWS].astype(F32)
         high, low = extra[0:1], extra[1:2]
         tops[...] = jnp.maximum(tops[...], extra[2:3])
-        for h in range(BW // 128):
-            key = jnp.where(high == h, low, -1.0)
-            hot = jnp.where(row_id == key, 1.0, 0.0).astype(BF16)
-            acc[:, h * 128 : (h + 1) * 128] += lax.dot_general(
+        for h in range(0, BW // 128, 2):
+            width = min(256, BW - h * 128)
+            hot = jnp.concatenate(
+                [
+                    jnp.where(row_id == jnp.where(high == h + u, low, -1.0), 1.0, 0.0).astype(BF16)
+                    for u in range(width // 128)
+                ],
+                axis=0,
+            )
+            acc[:, h * 128 : h * 128 + width] += lax.dot_general(
                 both[:LAGS], hot, (((1,), (1,)), ((), ())), preferred_element_type=F32
             )
 
-    route(1).wait_recv()
-    add(recv[0], recv[1])
-
-    def pair(g, carry):
-        i = 2 * g
-        route(i).wait_recv()
-        route(i + 1).wait_recv()
-        add(recv[i], recv[i + 1])
-        return carry
-
-    lax.fori_loop(1, NB // 2, pair, 0)
+    def pairs(h, carry):
+        for u in range(8):
+            i = 8 * h + u
+            if u == 0:
+
+                @pl.when(h > 0)
+                def _():
+                    route(i).wait_recv()
+
+            else:
+                route(i).wait_recv()
+        for u in range(4):
+            add(recv[8 * h + 2 * u], recv[8 * h + 2 * u + 1])
+        return carry
+
+    lax.fori_loop(0, NB // 8, pairs, 0)
 
     for h in range(BW // 128):
         fin[:, h, :] = acc[:, h * 128 : (h + 1) * 128]
@@ -330,7 +341,7 @@
     for j in range(32):
         out[9 * j : 9 * j + 9, :] = got[j, 0:9, :] + got[32 + j, 0:9, :]
         top = jnp.maximum(top, jnp.maximum(got[j, 9:10, :], got[32 + j, 9:10, :]))
-    most[...] = jnp.broadcast_to(top, (8, 128))
+    most[0, 0] = jnp.max(top).astype(jnp.int32)
 
     def drain(i, carry):
         route(i).wait_send()
@@ -364,7 +375,7 @@
 
 SUMS = (
     jax.ShapeDtypeStruct((32 * BW // 128, 128), F32),
-    jax.ShapeDtypeStruct((8, 128), F32),
+    jax.ShapeDtypeStruct((1, 1), jnp.int32),
 )
 
 
@@ -391,7 +402,7 @@
             pl.BlockSpec(memory_space=VMEM),
             pl.BlockSpec(memory_space=VMEM),
         ],
-        out_specs=(pl.BlockSpec(memory_space=VMEM),) * 2,
+        out_specs=(pl.BlockSpec(memory_space=VMEM), pl.BlockSpec(memory_space=SMEM)),
         scratch_shapes=[
             pltpu.VMEM((ROWS8, QUARTER), F32),
             pltpu.VMEM((ROWS8, QUARTER), F32),
@@ -691,7 +702,7 @@
             jax.ShapeDtypeStruct((ROWS8, QUARTER), jnp.int32),
         ),
         in_specs=[pl.BlockSpec(memory_space=SMEM)] + [hbm] * 10,
-        out_specs=(vmem, vmem, hbm, hbm),
+        out_specs=(vmem, pl.BlockSpec(memory_space=SMEM), hbm, hbm),
         scratch_shapes=[
             pltpu.VMEM((FB, ROWS8, W), BF16),
             pltpu.VMEM(plane, F32),
@@ -743,7 +754,7 @@
         smoothing_kernel, raw_frames, dark_frame, flat_field, pixel_gain, bin_labels,
         lag_list.reshape(1, LAGS), tables,
     )
-    needed = most[0, 0].astype(jnp.int32)
+    needed = most[0, 0]
 
     def more(state):
         return state[0] < needed

time: 97.1 us -> 93.9 us (0.967)
  Pallas kernels: 94.3 us -> 92.3 us
  local copies, waits for them, and re-layouts: 1.87 us -> 0.67 us
    pallas_call x1, Pallas kernels: 94.3 us -> 92.3 us  [first_round(): pl.pallas_call(main_kernel, out_shape=(*SUMS, jax.ShapeDtypeStruct((ROWS8...]
    slice x1 -> x0, local copies, waits for them, and re-layouts: 1.2 us -> none  [per_device(): needed = most[0, 0].astype(jnp.int32)]
where the time goes in v6:
time: 93.9 us; the launch traced here: 93.8 us
  Pallas kernels  92.3 us (98%)
    pallas_call x1, Pallas kernels, first_round(): pl.pallas_call(main_kernel, out_shape=(*SUMS, jax.ShapeDtypeStruct((ROWS8...  92.3 us

profile of v6, /device:TPU:1, one launch (start us, length us, event | category | flops | bytes accessed | tf_op | source)
XLA Modules:
  0.0 93.8 jit_solution(14163708750382956387)
XLA Ops:
  0.0 92.3 %first.1 = (f32[288,128]{1,0:T(8,128)S(1)}, s32[1,1]{1,0:T(1,128)}, bf16[8,72,512]{2,1,0:T(8,128)(2,1)S(1)}, s32[8,512]{1,0:T(8,128)S(1)}) custom-call(f32[5,5]{1,0:T(8,128)} %taps.1, bf16[80,8,2048]{2,1,0:T(8,128)(2,1)} %raw_in.1, f32[8,2048]{1,0:T(8,128)} %dark_in.1, f32[8,2048]{1,0:T(8,128)} %flat_in.1, f32[8,2048]{1,0:T(8,128)} %gain_in.1, ...), custom_call_target="tpu_custom_call" | custom-call | tf_op jit(solution)/shard_map/first/pallas_call | solution.py:697
  92.3 0.8 while.10
  93.1 0.7 copy.19
